TPU v7x, 256 devices: a whole 4x4x8 slice. The times are simulated.
256 devices in a mesh: dp: 16 (over y, z_lo, core), expert: 16 (over z_hi, x).
Axes of the slice: x: 4, y: 4, z: 8 (z_hi: 4, z_lo: 2; z = z_hi * 2 + z_lo), core: 2. Of those that a mesh axis runs over, the one named last changes fastest.
Arguments:
- tokens: bfloat16 [16384, 7168], P('expert', 'dp'), may hold values from -6 to 6
- expert_ids: int32 [16384, 8], P('expert'), may hold values from 0 to 255, all different within a row; in each aligned block of 1024 rows (0 to 1023, 1024 to 2047, ...) at most 64 rows name the same one
- gates: float32 [16384, 8], P('expert'), may hold values from 0.05 to 1
- gate_weight: bfloat16 [16, 7168, 2048], P('expert', 'dp'), may hold values from -0.0625 to 0.0625
- up_weight: bfloat16 [16, 7168, 2048], P('expert', 'dp'), may hold values from -0.0625 to 0.0625
- down_weight: bfloat16 [16, 2048, 7168], P('expert', None, 'dp'), may hold values from -0.125 to 0.125
- partner: int32 [16], replicated, may hold values from 0 to 15, as said below
- capacity: int32 [16], replicated, may hold values from 80 to 640, as said below
Outputs:
- mixed: bfloat16 [16384, 7168], P('expert', 'dp')
- placed_gate: bfloat16 [16, 7168, 2048], P('expert', 'dp')
- placed_up: bfloat16 [16, 7168, 2048], P('expert', 'dp')
- placed_down: bfloat16 [16, 2048, 7168], P('expert', None, 'dp')
Inputs may be any that keep to these rules, and one draw needn't show every extreme that they name: `expert_ids`: in every aligned block of 1024 rows no expert number is named by more than 64 rows. partner[partner[k]] == k for every slot k; 4 pairs of slots are exchanged, the other slots map to themselves. Some slot has capacity exactly 640.
All inputs are finite; a program needn't handle non-finite values.
Results may differ from a plain program's by a relative error of at most 0.0057.
Values may be sent and summed in bfloat16 or wider, within the bound.
A program may use at most 128 MiB of HBM per device.

v0:
```python
import jax
import jax.numpy as jnp
from jax import lax
from jax.sharding import PartitionSpec as P

MOST = 64
CAP_MAX = 640


def local(tokens, expert_ids, gates, gate_weight, up_weight, down_weight, partner, capacity):
    n_slots = lax.axis_size("expert")
    my_slot = lax.axis_index("expert")
    tok_rows, col_width = tokens.shape
    per_token = expert_ids.shape[1]
    slot_count = n_slots * MOST
    flat_ids = expert_ids.reshape(-1)
    flat_rows = jnp.arange(flat_ids.shape[0], dtype=jnp.int32) // per_token
    flat_gates = gates.reshape(-1)
    slot_numbers = jnp.arange(n_slots, dtype=jnp.int32)
    in_window = flat_ids < n_slots
    onehot = (flat_ids[:, None] == slot_numbers[None, :]) & in_window[:, None]
    onehot_int = onehot.astype(jnp.int32)
    local_rank = jnp.sum(jnp.where(onehot, jnp.cumsum(onehot_int, axis=0) - 1, 0), axis=1)
    counts = jnp.sum(onehot_int, axis=0)
    pieces = (
        lax.all_to_all(gate_weight, "expert", split_axis=1, concat_axis=0, tiled=True),
        lax.all_to_all(up_weight, "expert", split_axis=1, concat_axis=0, tiled=True),
        lax.all_to_all(down_weight, "expert", split_axis=1, concat_axis=0, tiled=True),
    )
    reordered = tuple((jnp.take(item, partner, axis=0) for item in pieces))
    placed_gate, placed_up, placed_down = (
        lax.all_to_all(reordered[0], "expert", split_axis=0, concat_axis=1, tiled=True),
        lax.all_to_all(reordered[1], "expert", split_axis=0, concat_axis=1, tiled=True),
        lax.all_to_all(reordered[2], "expert", split_axis=0, concat_axis=1, tiled=True),
    )
    my_limit = jnp.sum(jnp.where(slot_numbers == my_slot, capacity, 0))
    w_gate_all, w_up_all, w_down_all = (placed_gate, placed_up, placed_down)
    dest_flat = jnp.sum(jnp.where(onehot, partner[None, :], 0), axis=1)
    position = jnp.where(in_window, dest_flat * MOST + local_rank, slot_count)
    send_rows = (
        jnp.full((slot_count + 1,), tok_rows, jnp.int32).at[position].set(flat_rows)[:slot_count]
    )
    send_gates = jnp.zeros((slot_count + 1,), jnp.float32).at[position].set(flat_gates)[:slot_count]
    padded_tokens = jnp.concatenate([tokens, jnp.zeros((1, col_width), tokens.dtype)], axis=0)
    send_block = padded_tokens[send_rows].reshape(n_slots, MOST, col_width)
    counts_by_dest = jnp.zeros((n_slots,), jnp.int32).at[partner].set(counts)
    received, recv_counts = (
        lax.all_to_all(send_block, "expert", split_axis=0, concat_axis=0, tiled=True),
        lax.all_to_all(counts_by_dest[:, None], "expert", split_axis=0, concat_axis=0, tiled=True),
    )
    source_counts = recv_counts[:, 0]
    offsets = jnp.cumsum(source_counts) - source_counts
    slot_number = jnp.arange(MOST, dtype=jnp.int32)
    global_rank = offsets[:, None] + slot_number[None, :]
    kept_mask = (slot_number[None, :] < source_counts[:, None]) & (global_rank < my_limit)
    slot_place = jnp.where(kept_mask, global_rank, CAP_MAX).reshape(-1).astype(jnp.int32)
    source_index = (
        jnp.full((CAP_MAX + 1,), slot_count, jnp.int32)
        .at[slot_place]
        .set(jnp.arange(slot_count, dtype=jnp.int32))[:CAP_MAX]
    )
    received_flat = jnp.concatenate(
        [received.reshape(slot_count, col_width), jnp.zeros((1, col_width), received.dtype)], axis=0
    )
    picked = received_flat[source_index]
    gate_part = jnp.dot(picked, w_gate_all[0], preferred_element_type=jnp.float32)
    up_part = jnp.dot(picked, w_up_all[0], preferred_element_type=jnp.float32)
    w_down_local = w_down_all[0]
    gate_sum, up_sum = (
        lax.psum_scatter(gate_part, "dp", scatter_dimension=1, tiled=True),
        lax.psum_scatter(up_part, "dp", scatter_dimension=1, tiled=True),
    )
    hidden = (jax.nn.silu(gate_sum) * up_sum).astype(jnp.bfloat16)
    expert_out = jnp.dot(
        lax.all_gather(hidden, "dp", axis=1, tiled=True),
        w_down_local,
        preferred_element_type=jnp.float32,
    ).astype(jnp.bfloat16)
    padded_out = jnp.concatenate([expert_out, jnp.zeros((1, col_width), jnp.bfloat16)], axis=0)
    reply = padded_out[slot_place].reshape(n_slots, MOST, col_width)
    returned_rows = lax.all_to_all(reply, "expert", split_axis=0, concat_axis=0, tiled=True)
    weighted = (
        returned_rows.reshape(slot_count, col_width).astype(jnp.float32) * send_gates[:, None]
    )
    result = (
        jnp.zeros((tok_rows + 1, col_width), jnp.float32).at[send_rows].add(weighted)[:tok_rows]
    )
    return (result.astype(jnp.bfloat16), placed_gate, placed_up, placed_down)


def solution(mesh):
    return jax.shard_map(
        local,
        mesh=mesh,
        in_specs=(
            P("expert", "dp"),
            P("expert", None),
            P("expert", None),
            P("expert", "dp", None),
            P("expert", "dp", None),
            P("expert", None, "dp"),
            P(),
            P(),
        ),
        out_specs=(
            P("expert", "dp"),
            P("expert", "dp", None),
            P("expert", "dp", None),
            P("expert", None, "dp"),
        ),
        check_vma=False,
    )
```

profile of v0, /device:TPU:57, one launch (start us, length us, event | category | flops | bytes accessed | tf_op | source)
XLA Modules:
  0.0 652.0 jit_solution(7636263825429411234)
XLA Ops:
  8.7 4.8 reduce-window.18
  16.5 9.9 %all-to-all-start.1 = ((s32[16,1,1]{2,1,0:T(1,128)}), s32[16,1,1]{2,1,0:T(1,128)S(1)}, u32[]{:S(2)}, u32[]{:S(2)}) async-start(s32[16,1,1]{2,1,0:T(1,128)} %copy.55), calls=%async_computation.1 | async-start | bytes 16384 | tf_op jit(solution)/shard_map/all_to_all | solution.py:49
  26.4 6.1 copy.85
  33.0 11.6 %reduce.8 = bf16[448,2048]{1,0:T(8,128)(2,1)S(1)} reduce(bf16[448,1,2048]{2,1,0:T(2,128)(2,1)} %bitcast.55, bf16[]{:T(256)} %broadcast.238), dimensions={1}, to_apply=%bitcast.51.reduce_sub_computation | reduce | bytes 3670018
  44.6 3.2 reshape.345
  47.8 9.8 %all-to-all-start.2 = ((bf16[16,2,28672]{2,1,0:T(2,128)(2,1)}), bf16[16,2,28672]{2,1,0:T(2,128)(2,1)}, u32[]{:S(2)}, u32[]{:S(2)}) async-start(bf16[16,2,28672]{2,1,0:T(2,128)(2,1)} %reshape.345), calls=%async_computation.2 | async-start | bytes 3670016 | tf_op jit(solution)/shard_map/all_to_all | solution.py:26
  57.6 4.6 copy.84
  62.2 11.6 %reduce.9 = bf16[448,2048]{1,0:T(8,128)(2,1)S(1)} reduce(bf16[448,1,2048]{2,1,0:T(2,128)(2,1)} %bitcast.56, bf16[]{:T(256)} %broadcast.238), dimensions={1}, to_apply=%bitcast.50.reduce_sub_computation | reduce | bytes 3670018
  73.8 3.2 reshape.343
  77.0 26.7 %all-to-all-done.2 = bf16[16,2,28672]{2,1,0:T(2,128)(2,1)} async-done(((bf16[16,2,28672]{2,1,0:T(2,128)(2,1)}), bf16[16,2,28672]{2,1,0:T(2,128)(2,1)}, u32[]{:S(2)}, u32[]{:S(2)}) %all-to-all-start.2) | async-done | bytes 1835040 | tf_op jit(solution)/shard_map/all_to_all | solution.py:26
  103.7 4.4 all-to-all-start.4
  109.5 30.4 %scatter_custom_fusion = s32[1025]{0:T(1024)S(1)} fusion(s32[8192]{0:T(1024)S(1)} %bitcast.65, s32[8192]{0:T(1024)S(1)} %add_select_fusion, s32[]{:T(128)} %constant.31.clone.1), kind=kCustom, calls=%fused_computation.58 | custom fusion | bytes 4104 | tf_op jit(solution)/shard_map/scatter | solution.py:41
  140.0 5.1 gather_fusion
  145.1 10.2 %reshape.346 = bf16[448,1,2048]{2,1,0:T(2,128)(2,1)} reshape(bf16[16,2,28672]{2,1,0:T(2,128)(2,1)} %all-to-all-done.2) | data formatting | bytes 3670016
  156.9 7.5 %all-to-all-start = ((bf16[16,64,448]{2,1,0:T(8,128)(2,1)}), bf16[16,64,448]{2,1,0:T(8,128)(2,1)S(1)}, u32[]{:S(2)}, u32[]{:S(2)}) async-start(bf16[16,64,448]{2,1,0:T(8,128)(2,1)} %bitcast.3), calls=%async_computation | async-start | bytes 2097152 | tf_op jit(solution)/shard_map/all_to_all | solution.py:48
  164.4 12.6 %bitcast_reduce_fusion = bf16[448,2048]{1,0:T(8,128)(2,1)} fusion(bf16[448,1,2048]{2,1,0:T(2,128)(2,1)} %reshape.346), kind=kLoop, calls=%fused_computation.70 | loop fusion | bytes 3670016 | tf_op jit(solution)/shard_map/all_to_all | solution.py:26
  179.4 10.2 %reshape.344 = bf16[448,1,2048]{2,1,0:T(2,128)(2,1)} reshape(bf16[16,2,28672]{2,1,0:T(2,128)(2,1)} %all-to-all-done.4) | data formatting | bytes 3670016
  189.6 12.6 %bitcast_reduce_fusion.1 = bf16[448,2048]{1,0:T(8,128)(2,1)} fusion(bf16[448,1,2048]{2,1,0:T(2,128)(2,1)} %reshape.344), kind=kLoop, calls=%fused_computation.71 | loop fusion | bytes 3670016 | tf_op jit(solution)/shard_map/all_to_all | solution.py:27
  202.2 3.5 all_to_all.73
  207.8 3.8 gather_fusion.5
  211.6 4.0 broadcast_select_fusion.1
  216.6 9.2 %all-to-all-start.5 = ((bf16[16,28,2048]{2,1,0:T(8,128)(2,1)}), bf16[16,28,2048]{2,1,0:T(8,128)(2,1)S(1)}, u32[]{:S(2)}, u32[]{:S(2)}) async-start(bf16[16,28,2048]{2,1,0:T(8,128)(2,1)} %get-tuple-element.27), calls=%async_computation.6 | async-start | bytes 4194304 | tf_op jit(solution)/shard_map/all_to_all | solution.py:33
  228.0 4.3 scatter_custom_fusion.2
  233.7 3.3 gather_fusion.1
  237.0 42.7 %all-to-all-done.5 = bf16[16,28,2048]{2,1,0:T(8,128)(2,1)S(1)} async-done(((bf16[16,28,2048]{2,1,0:T(8,128)(2,1)}), bf16[16,28,2048]{2,1,0:T(8,128)(2,1)S(1)}, u32[]{:S(2)}, u32[]{:S(2)}) %all-to-all-start.5) | async-done | bytes 1835040 | tf_op jit(solution)/shard_map/all_to_all | solution.py:33
  281.1 5.3 fusion.27
  286.5 66.8 %all_to_all.91 = bf16[16,28,2048]{2,1,0:T(8,128)(2,1)} all-to-all(bf16[16,28,2048]{2,1,0:T(8,128)(2,1)} %get-tuple-element.26), channel_id=1, replica_groups=mesh['dp'=16,'expert'=16] {'expert'}, dimensions={0} | all-to-all | bytes 3670016 | tf_op jit(solution)/shard_map/all_to_all | solution.py:32
  353.3 3.6 squeeze.10
  356.9 5.4 fusion.26
  362.3 10.8 %copy.59 = bf16[1,2048,448]{2,0,1:T(2,128)(2,1)} copy(bf16[1,2048,448]{1,2,0:T(8,128)(2,1)} %param.15) | data formatting | bytes 3670016 | tf_op args[5]
  373.1 15.4 %reduce.10 = bf16[2048,448]{1,0:T(8,128)(2,1)} reduce(bf16[2048,1,448]{2,1,0:T(2,128)(2,1)} %bitcast.53, bf16[]{:T(256)} %broadcast.238), dimensions={1}, to_apply=%bitcast.36.reduce_sub_computation | reduce | bytes 3670018
  388.4 5.8 reshape.347
  394.2 4.4 all-to-all-start.6
  401.4 92.9 %reduce-scatter.3.cloned.1.call-done = f32[640,128]{1,0:T(8,128)} async-done(((f32[640,2048]{1,0:T(8,128)}), f32[640,128]{1,0:T(8,128)}) %reduce-scatter.3.cloned.1.call-update) | async-done | bytes 327696 | tf_op jit(solution)/shard_map/reduce_scatter | solution.py:70
  496.2 10.8 %reshape.348 = bf16[2048,1,448]{2,1,0:T(2,128)(2,1)} reshape(bf16[16,2,28672]{2,1,0:T(2,128)(2,1)} %all-to-all-done.6) | data formatting | bytes 3670016
  506.9 4.3 copy.71
  511.2 3.9 copy.61
  515.1 3.5 gather_fusion.2
  521.7 7.4 %all-to-all-start.7 = ((bf16[16,128,448]{1,2,0:T(8,128)(2,1)}), bf16[16,128,448]{1,2,0:T(8,128)(2,1)}, u32[]{:S(2)}, u32[]{:S(2)}) async-start(bf16[16,128,448]{1,2,0:T(8,128)(2,1)} %broadcast_select_fusion.2), calls=%async_computation.9 | async-start | bytes 3670016 | tf_op jit(solution)/shard_map/all_to_all | solution.py:34
  529.1 42.7 %all-to-all-done.7 = bf16[16,128,448]{1,2,0:T(8,128)(2,1)} async-done(((bf16[16,128,448]{1,2,0:T(8,128)(2,1)}), bf16[16,128,448]{1,2,0:T(8,128)(2,1)}, u32[]{:S(2)}, u32[]{:S(2)}) %all-to-all-start.7) | async-done | bytes 1835040 | tf_op jit(solution)/shard_map/all_to_all | solution.py:34
  571.8 3.9 fusion.4
  576.1 5.1 gather_fusion.3
  581.2 6.4 all-to-all-start.8
  589.8 30.7 %scatter_custom_fusion.3 = f32[1025]{0:T(1024)S(1)} fusion(s32[8192]{0:T(1024)S(1)} %bitcast.66, f32[8192]{0:T(1024)S(1)} %reshape.304, f32[]{:T(128)} %constant.30.clone.1), kind=kCustom, calls=%fused_computation.56 | custom fusion | bytes 4104 | tf_op jit(solution)/shard_map/scatter | solution.py:43
  620.5 3.9 copy.62
  624.4 3.9 all_to_all.81
  628.3 3.6 all_to_all.79
  633.3 8.9 %scatter_custom_fusion.4 = f32[1025,448]{1,0:T(8,128)} fusion(s32[1024]{0:T(1024)S(1)} %get-tuple-element.25, bf16[1024,448]{1,0:T(8,128)(2,1)S(1)} %bitcast.60, f32[]{:T(128)} %constant.30.clone.1, f32[1024]{0:T(1024)S(1)} %slice-done), kind=kCustom, calls=%fused_computation.13 | custom fusion | flops 1376256 | bytes 2889476 | tf_op jit(solution)/shard_map/scatter-add | solution.py:86
  (87 shorter events, 33.0 us)
Async XLA Ops:
  8.1 6.3 copy-start.8
  16.5 31.3 %all-to-all-start.1 = ((s32[16,1,1]{2,1,0:T(1,128)}), s32[16,1,1]{2,1,0:T(1,128)S(1)}, u32[]{:S(2)}, u32[]{:S(2)}) async-start(s32[16,1,1]{2,1,0:T(1,128)} %copy.55), calls=%async_computation.1 | async-start | bytes 16384 | tf_op jit(solution)/shard_map/all_to_all | solution.py:49
  47.8 9.8 %copy-start.2 = (bf16[1,448,2048]{2,1,0:T(8,128)(2,1)S(1)}, bf16[1,448,2048]{2,1,0:T(8,128)(2,1)}, u32[]{:S(2)}) copy-start(bf16[1,448,2048]{2,1,0:T(8,128)(2,1)} %param.14) | copy-start | bytes 5505028
  47.8 55.9 %all-to-all-start.2 = ((bf16[16,2,28672]{2,1,0:T(2,128)(2,1)}), bf16[16,2,28672]{2,1,0:T(2,128)(2,1)}, u32[]{:S(2)}, u32[]{:S(2)}) async-start(bf16[16,2,28672]{2,1,0:T(2,128)(2,1)} %reshape.345), calls=%async_computation.2 | async-start | bytes 3670016 | tf_op jit(solution)/shard_map/all_to_all | solution.py:26
  77.0 31.1 %copy-start.5 = (s32[1024,8]{0,1:T(8,128)S(1)}, s32[1024,8]{0,1:T(8,128)}, u32[]{:S(2)}) copy-start(s32[1024,8]{0,1:T(8,128)} %param.11) | copy-start | bytes 98308
  77.0 31.7 %copy-start.3 = (bf16[1024,448]{0,1:T(8,128)(2,1)S(1)}, bf16[1024,448]{0,1:T(8,128)(2,1)}, u32[]{:S(2)}) copy-start(bf16[1024,448]{0,1:T(8,128)(2,1)} %param.10) | copy-start | bytes 2752516
  103.7 53.3 %all-to-all-start.4 = ((bf16[16,2,28672]{2,1,0:T(2,128)(2,1)}), bf16[16,2,28672]{2,1,0:T(2,128)(2,1)}, u32[]{:S(2)}, u32[]{:S(2)}) async-start(bf16[16,2,28672]{2,1,0:T(2,128)(2,1)} %reshape.343), calls=%async_computation.5 | async-start | bytes 3670016 | tf_op jit(solution)/shard_map/all_to_all | solution.py:27
  156.9 58.7 %all-to-all-start = ((bf16[16,64,448]{2,1,0:T(8,128)(2,1)}), bf16[16,64,448]{2,1,0:T(8,128)(2,1)S(1)}, u32[]{:S(2)}, u32[]{:S(2)}) async-start(bf16[16,64,448]{2,1,0:T(8,128)(2,1)} %bitcast.3), calls=%async_computation | async-start | bytes 2097152 | tf_op jit(solution)/shard_map/all_to_all | solution.py:48
  207.8 3.8 copy-start
  215.6 1.0 copy-start.1
  215.6 10.2 %copy-start.9 = (s32[16]{0:T(128)S(1)}, s32[16]{0:T(128)}, u32[]{:S(2)}) copy-start(s32[16]{0:T(128)} %param.17) | copy-start | bytes 196
  216.6 63.1 %all-to-all-start.5 = ((bf16[16,28,2048]{2,1,0:T(8,128)(2,1)}), bf16[16,28,2048]{2,1,0:T(8,128)(2,1)S(1)}, u32[]{:S(2)}, u32[]{:S(2)}) async-start(bf16[16,28,2048]{2,1,0:T(8,128)(2,1)} %get-tuple-element.27), calls=%async_computation.6 | async-start | bytes 4194304 | tf_op jit(solution)/shard_map/all_to_all | solution.py:33
  225.7 175.6 %reduce-scatter.5.cloned.1.call-start = ((), (), s32[]{:S(2)}) async-start(), calls=%async_computation.12 | async-start | bytes 5570560 | tf_op jit(solution)/shard_map/reduce_scatter | solution.py:71
  237.0 44.2 %copy-start.4 = (bf16[640,448]{1,0:T(8,128)(2,1)S(1)}, bf16[640,448]{1,0:T(8,128)(2,1)}, u32[]{:S(2)}) copy-start(bf16[640,448]{1,0:T(8,128)(2,1)} %gather_fusion.1) | copy-start | bytes 1720324
  286.5 207.8 %reduce-scatter.3.cloned.1.call-start = ((), (), s32[]{:S(2)}) async-start(), calls=%async_computation.11 | async-start | bytes 5570560 | tf_op jit(solution)/shard_map/reduce_scatter | solution.py:70
  394.2 102.0 %all-to-all-start.6 = ((bf16[16,2,28672]{2,1,0:T(2,128)(2,1)}), bf16[16,2,28672]{2,1,0:T(2,128)(2,1)}, u32[]{:S(2)}, u32[]{:S(2)}) async-start(bf16[16,2,28672]{2,1,0:T(2,128)(2,1)} %reshape.347), calls=%async_computation.8 | async-start | bytes 3670016 | tf_op jit(solution)/shard_map/all_to_all | solution.py:28
  398.6 173.2 %all-gather.2.cloned.1.call-start = ((), (), s32[]{:S(2)}) async-start(), calls=%async_computation.13 | async-start | bytes 2785280 | tf_op jit(solution)/shard_map/all_gather | solution.py:75
  521.7 50.2 %all-to-all-start.7 = ((bf16[16,128,448]{1,2,0:T(8,128)(2,1)}), bf16[16,128,448]{1,2,0:T(8,128)(2,1)}, u32[]{:S(2)}, u32[]{:S(2)}) async-start(bf16[16,128,448]{1,2,0:T(8,128)(2,1)} %broadcast_select_fusion.2), calls=%async_computation.9 | async-start | bytes 3670016 | tf_op jit(solution)/shard_map/all_to_all | solution.py:34
  581.1 6.4 copy-start.6
  581.2 52.1 %all-to-all-start.8 = ((bf16[16,64,448]{2,1,0:T(8,128)(2,1)}), bf16[16,64,448]{2,1,0:T(8,128)(2,1)S(1)}, u32[]{:S(2)}, u32[]{:S(2)}) async-start(bf16[16,64,448]{2,1,0:T(8,128)(2,1)} %bitcast.58), calls=%async_computation.10 | async-start | bytes 2097152 | tf_op jit(solution)/shard_map/all_to_all | solution.py:81
  620.5 7.8 %copy-start.7 = (f32[1025]{0:T(1024)}, f32[1025]{0:T(1024)S(1)}, u32[]{:S(2)}) copy-start(f32[1025]{0:T(1024)S(1)} %scatter_custom_fusion.3) | copy-start | bytes 12304
  631.9 1.4 slice-start
Sparse Core Ops, SparseCore 0:
  286.6 114.7 reduce-scatter.4
  403.9 90.3 reduce-scatter.2
  496.7 50.4 all-gather.1
where the time goes:
time: 665 us; the launch traced here: 652 us
  local copies, waits for them, and re-layouts  223 us (34%)
  waiting for transfers between devices  209 us (31%)
  blocking collectives  66.8 us (10%)
  other arithmetic  64.5 us (10%)
  starting transfers between devices  59 us (9%)
  matrix products  14.6 us (2%)
  between operations  14.4 us (2%)
    reduce_scatter x1, waiting for transfers between devices, local(): lax.psum_scatter(gate_part, 'dp', scatter_dimension=1, tiled=True)  92.9 us
    unnamed x36, local copies, waits for them, and re-layouts  74.6 us
    all_to_all x1, blocking collectives, local(): lax.all_to_all(reordered[0], 'expert', split_axis=0, concat_axis=1, tiled...  66.8 us
    all_to_all x1, waiting for transfers between devices, local(): lax.all_to_all(reordered[1], 'expert', split_axis=0, concat_axis=1, tiled...  42.7 us
    all_to_all x1, waiting for transfers between devices, local(): lax.all_to_all(reordered[2], 'expert', split_axis=0, concat_axis=1, tiled...  42.7 us
    unnamed x3, other arithmetic  38.6 us
    scatter x1, local copies, waits for them, and re-layouts, local(): jnp.zeros((slot_count + 1,), jnp.float32).at[position].set(flat_gates)  30.7 us
    scatter x1, local copies, waits for them, and re-layouts, local(): jnp.full((slot_count + 1,), tok_rows, jnp.int32).at[position].set(flat_rows)  30.4 us
  transfers between devices with their start and end apart: 11, of which 6 were waited for; matrix products, arithmetic and copies ran while one was open for 38% of the time, Pallas kernels for 0%

commit v1 on v0

v1 whole, which is shorter than its diff:
```python
import functools

import jax
import jax.numpy as jnp
from jax import lax
from jax.experimental import pallas as pl
from jax.experimental.pallas import tpu as pltpu
from jax.sharding import PartitionSpec as P

MOST = 64
CAP = 640
N = 16
MESH = pl.DeviceIdType.MESH
F32 = jnp.float32
BF16 = jnp.bfloat16
I32 = jnp.int32


def iota(shape, axis):
    return lax.broadcasted_iota(I32, shape, axis)


def rcopy(src, dst, send, recv, dev):
    return pltpu.make_async_remote_copy(
        src_ref=src, dst_ref=dst, send_sem=send, recv_sem=recv, device_id=dev, device_id_type=MESH
    )


def kernel(
    ids, gates, lim, partner, tok_h, wg_h, wu_h, wd_h,
    mixed, pg, pu, pd,
    tok, wg, wu, wd, key, gat, whi, wlo,
    xs, xr, cs, cr, offs, pm, picked,
    cbs, cbr, acc, y1s, y1r, y2s, y2r, zs, zr, hid, eo, rs, rr,
    w1g, w1u, w1d, w2g, w2u, w2d,
    loc, loc1, loc2, w1ss, w1rs, w2ss, w2rs, xss, xrs, css, crs, rss, rrs, dss, drs,
):
    tokens, width = tok_h.shape
    me = lax.axis_index("expert")
    dp = lax.axis_index("dp")
    yy, zl, cc = lax.div(dp, 4), lax.rem(lax.div(dp, 2), 2), lax.rem(dp, 2)

    def at_y(v):
        return v * 4 + zl * 2 + cc

    ya = yy + 1 - 2 * lax.rem(yy, 2)
    yb = 3 - yy
    yc = lax.rem(yy + 2, 4)
    dev_c = {"dp": dp + 1 - 2 * cc}
    dev_z = {"dp": dp + 2 - 4 * zl}
    dev_ya = {"dp": at_y(ya)}
    dev_yb = {"dp": at_y(yb)}

    loads = [
        pltpu.make_async_copy(tok_h, tok, loc.at[0]),
        pltpu.make_async_copy(wg_h.at[0], wg, loc.at[1]),
        pltpu.make_async_copy(wu_h.at[0], wu, loc.at[2]),
        pltpu.make_async_copy(wd_h.at[0], wd, loc.at[3]),
    ]
    for c in loads:
        c.start()

    barrier = pltpu.get_barrier_semaphore()

    def hello(t, _):
        pl.semaphore_signal(barrier, inc=1, device_id={"expert": lax.rem(me + t, N)}, device_id_type=MESH)
        return 0

    lax.fori_loop(1, N, hello, 0)
    for d in (dev_c, dev_z, dev_ya, dev_yb):
        pl.semaphore_signal(barrier, inc=1, device_id=d, device_id_type=MESH)
    pl.semaphore_wait(barrier, N - 1 + 4)

    def cols(i, n=128):
        return pl.ds(pl.multiple_of(i * n, n), n)

    def w1(i, k, dst):
        c = cols(i)
        return (
            rcopy(wg_h.at[0, :, c], w1g.at[dst], w1ss.at[0, k], w1rs.at[0, dst], {"expert": i}),
            rcopy(wu_h.at[0, :, c], w1u.at[dst], w1ss.at[1, k], w1rs.at[1, dst], {"expert": i}),
            rcopy(wd_h.at[0, c, :], w1d.at[dst], w1ss.at[2, k], w1rs.at[2, dst], {"expert": i}),
        )

    def w1_send(t, _):
        i = lax.rem(me + t, N)
        for c in w1(i, t, me):
            c.start()
        return 0

    lax.fori_loop(1, N, w1_send, 0)
    mine = cols(me)
    w1_local = (
        pltpu.make_async_copy(wg_h.at[0, :, mine], w1g.at[me], loc1.at[0]),
        pltpu.make_async_copy(wu_h.at[0, :, mine], w1u.at[me], loc1.at[1]),
        pltpu.make_async_copy(wd_h.at[0, mine, :], w1d.at[me], loc1.at[2]),
    )
    for c in w1_local:
        c.start()

    e_of = iota((N, tokens), 0)
    named = jnp.zeros((N, tokens), I32)
    gate = jnp.zeros((N, tokens), F32)
    for j in range(ids.shape[0]):
        eq = ids[j : j + 1, :] == e_of
        named = jnp.where(eq, 1, named)
        gate = jnp.where(eq, gates[j : j + 1, :], gate)
    run = named
    lane = iota((N, tokens), 1)
    step = 1
    while step < tokens:
        run = run + jnp.where(lane >= step, pltpu.roll(run, step, 1), 0)
        step *= 2
    key[...] = jnp.where(named > 0, run - 1, -1)
    gat[...] = gate

    loads[0].wait()
    row_of = iota((MOST, tokens), 0)

    def dispatch(t, _):
        e = lax.rem(me + t, N)
        krow = key[pl.ds(e, 1), :]
        pick = (row_of == krow).astype(F32).astype(BF16)
        rows = jnp.dot(pick, tok[...], preferred_element_type=F32).astype(BF16)
        total = jnp.sum(jnp.where(krow >= 0, 1.0, 0.0), axis=1, keepdims=True)
        total = jnp.broadcast_to(total, (8, 128))

        @pl.when(t > 0)
        def _():
            xs[e] = rows
            cs[e] = total
            rcopy(cs.at[e], cr.at[me], css.at[t], crs.at[me], {"expert": e}).start()
            rcopy(xs.at[e], xr.at[me], xss.at[t], xrs.at[me], {"expert": e}).start()

        @pl.when(t == 0)
        def _():
            xr[e] = rows
            cr[e] = total

        return 0

    lax.fori_loop(0, N, dispatch, 0)

    def spread(e, _):
        krow = key[pl.ds(e, 1), :]
        full = jnp.where(row_of == krow, gat[pl.ds(e, 1), :], 0.0)
        hi = full.astype(BF16)
        at = pl.ds(pl.multiple_of(e * MOST, MOST), MOST)
        whi[at, :] = hi
        wlo[at, :] = (full - hi.astype(F32)).astype(BF16)
        return 0

    lax.fori_loop(0, N, spread, 0)

    def x_wait(t, _):
        b = lax.rem(me + t, N)
        rcopy(cs.at[b], cr.at[b], css.at[t], crs.at[b], {"expert": b}).wait_recv()
        rcopy(xs.at[b], xr.at[b], xss.at[t], xrs.at[b], {"expert": b}).wait_recv()
        return 0

    lax.fori_loop(1, N, x_wait, 0)

    limit = lim[0:1, 0:1]
    p_of = iota((CAP, 2 * MOST), 0).astype(F32)
    l_of = iota((CAP, 2 * MOST), 1)
    i_of = lax.rem(l_of, MOST).astype(F32)

    def place(q, off):
        c0, c1 = cr[2 * q][0:1, 0:1], cr[2 * q + 1][0:1, 0:1]
        offs[2 * q] = jnp.broadcast_to(off, (8, 128))
        offs[2 * q + 1] = jnp.broadcast_to(off + c0, (8, 128))
        count = jnp.where(l_of < MOST, c0, c1)
        start = jnp.where(l_of < MOST, off, off + c0)
        hit = (p_of == start + i_of) & (i_of < count) & (p_of < limit)
        pm[:, cols(q)] = jnp.where(hit, 1.0, 0.0).astype(BF16)
        return off + c0 + c1

    lax.fori_loop(0, N // 2, place, jnp.zeros((1, 1), F32))
    picked[...] = jnp.dot(
        pm[...], xr[...].reshape(N * MOST, width), preferred_element_type=F32
    ).astype(BF16)

    half = wg.shape[1] // 2
    loads[1].wait()
    loads[2].wait()

    def theirs(j, _):
        for w, ref in enumerate((wg, wu)):
            at = pl.ds(pl.multiple_of((1 - cc) * half + j * 256, 256), 256)
            cbs[w, :, cols(j, 256)] = jnp.dot(
                picked[...], ref[:, at], preferred_element_type=F32
            ).astype(BF16)
        return 0

    def ours(j, _):
        for w, ref in enumerate((wg, wu)):
            at = pl.ds(pl.multiple_of(cc * half + j * 256, 256), 256)
            acc[w, :, cols(j, 256)] = jnp.dot(picked[...], ref[:, at], preferred_element_type=F32)
        return 0

    lax.fori_loop(0, half // 256, theirs, 0)
    to_c = rcopy(cbs, cbr, dss.at[0], drs.at[0], dev_c)
    to_c.start()
    lax.fori_loop(0, half // 256, ours, 0)
    to_c.wait_recv()

    def block(w, q):
        at = cols(q, 256)
        return acc[w, :, at] + cbr[w, :, at].astype(F32)

    y1 = []
    for w, (q, dev) in enumerate(((ya, dev_ya), (yb, dev_yb))):
        y1s[w, 0] = block(w, q).astype(BF16)
        y1s[w, 1] = block(w, yc).astype(BF16)
        c = rcopy(y1s.at[w], y1r.at[w], dss.at[1 + w], drs.at[1 + w], dev)
        c.start()
        y1.append(c)
    y2 = []
    for w, (q, dev) in enumerate(((yb, dev_yb), (ya, dev_ya))):
        y1[w].wait_recv()
        y2s[w] = (block(w, q) + y1r[w, 1].astype(F32)).astype(BF16)
        c = rcopy(y2s.at[w], y2r.at[w], dss.at[3 + w], drs.at[3 + w], dev)
        c.start()
        y2.append(c)
    for w in range(2):
        acc[w, :, cols(yy, 256)] = block(w, yy) + y1r[w, 0].astype(F32)
    for w in range(2):
        y2[w].wait_recv()
        y2f = y2r[w].astype(F32)
        lo, hi = y2f[:, :128], y2f[:, 128:]
        away = pl.ds(pl.multiple_of(yy * 256 + (1 - zl) * 128, 128), 128)
        here = pl.ds(pl.multiple_of(yy * 256 + zl * 128, 128), 128)
        zs[w] = (acc[w, :, away] + jnp.where(zl == 0, hi, lo)).astype(BF16)
        acc[w, :, here] = acc[w, :, here] + jnp.where(zl == 0, lo, hi)
    to_z = rcopy(zs, zr, dss.at[5], drs.at[5], dev_z)
    to_z.start()
    to_z.wait_recv()
    here = pl.ds(pl.multiple_of(yy * 256 + zl * 128, 128), 128)
    gsum = acc[0, :, here] + zr[0].astype(F32)
    usum = acc[1, :, here] + zr[1].astype(F32)
    own = cols(cc * 8 + yy * 2 + zl)
    hid[:, own] = (gsum / (1.0 + jnp.exp(-gsum)) * usum).astype(BF16)

    def chunk(c, q):
        return cols(c * 4 + q, 256)

    h_z = rcopy(hid.at[:, own], hid.at[:, own], dss.at[6], drs.at[6], dev_z)
    h_z.start()
    h_z_in = cols(cc * 8 + yy * 2 + 1 - zl)
    rcopy(hid.at[:, h_z_in], hid.at[:, h_z_in], dss.at[6], drs.at[6], dev_z).wait_recv()
    me_q = chunk(cc, yy)

    def to(at, k, dev):
        return rcopy(hid.at[at[0], at[1]], hid.at[at[0], at[1]], dss.at[k], drs.at[k], dev)

    everyrow, top, low = pl.ds(0, CAP), pl.ds(0, CAP // 2), pl.ds(CAP // 2, CAP // 2)
    h_ya = to((everyrow, me_q), 7, dev_ya)
    h_yb = to((everyrow, me_q), 8, dev_yb)
    h_ya.start()
    h_yb.start()
    h_c0 = to((everyrow, me_q), 9, dev_c)
    h_c0.start()
    to((everyrow, chunk(cc, ya)), 7, dev_ya).wait_recv()
    h_fa = to((top, chunk(cc, ya)), 10, dev_yb)
    h_fa.start()
    h_c1 = to((everyrow, chunk(cc, ya)), 11, dev_c)
    h_c1.start()
    to((everyrow, chunk(cc, yb)), 8, dev_yb).wait_recv()
    h_fb = to((low, chunk(cc, yb)), 12, dev_ya)
    h_fb.start()
    h_c2 = to((everyrow, chunk(cc, yb)), 13, dev_c)
    h_c2.start()
    to((top, chunk(cc, yc)), 10, dev_yb).wait_recv()
    to((low, chunk(cc, yc)), 12, dev_ya).wait_recv()
    h_c3 = to((everyrow, chunk(cc, yc)), 14, dev_c)
    h_c3.start()
    to((everyrow, chunk(1 - cc, yy)), 9, dev_c).wait_recv()
    to((everyrow, chunk(1 - cc, ya)), 11, dev_c).wait_recv()
    to((everyrow, chunk(1 - cc, yb)), 13, dev_c).wait_recv()
    to((everyrow, chunk(1 - cc, yc)), 14, dev_c).wait_recv()

    loads[3].wait()
    eo[...] = jnp.dot(hid[...], wd[...], preferred_element_type=F32).astype(BF16)

    i_row = iota((MOST, CAP), 0).astype(F32)
    p_lane = iota((MOST, CAP), 1).astype(F32)

    def reply(t, _):
        b = lax.rem(me + t, N)
        count, start = cr[b][0:1, 0:1], offs[b][0:1, 0:1]
        hit = (p_lane == start + i_row) & (i_row < count) & (p_lane < limit)
        rows = jnp.dot(
            jnp.where(hit, 1.0, 0.0).astype(BF16), eo[...], preferred_element_type=F32
        ).astype(BF16)

        @pl.when(t > 0)
        def _():
            rs[b] = rows
            rcopy(rs.at[b], rr.at[me], rss.at[t], rrs.at[me], {"expert": b}).start()

        @pl.when(t == 0)
        def _():
            rr[b] = rows

        return 0

    lax.fori_loop(0, N, reply, 0)

    for c in w1_local:
        c.wait()

    def w1_wait(t, _):
        s = lax.rem(me + t, N)
        for c in w1(me, t, s):
            c.wait_recv()
        return 0

    lax.fori_loop(1, N, w1_wait, 0)

    def w2(k, t, i):
        c = cols(i)
        return (
            rcopy(w2g.at[k], pg.at[0, :, c], w2ss.at[0, t], w2rs.at[0, i], {"expert": k}),
            rcopy(w2u.at[k], pu.at[0, :, c], w2ss.at[1, t], w2rs.at[1, i], {"expert": k}),
            rcopy(w2d.at[k], pd.at[0, c, :], w2ss.at[2, t], w2rs.at[2, i], {"expert": k}),
        )

    def w2_send(t, _):
        k = lax.rem(me + t, N)
        s = partner[k]
        w2g[k] = w1g[s]
        w2u[k] = w1u[s]
        w2d[k] = w1d[s]

        @pl.when(t > 0)
        def _():
            for c in w2(k, t, me):
                c.start()

        return 0

    lax.fori_loop(0, N, w2_send, 0)
    w2_local = (
        pltpu.make_async_copy(w2g.at[me], pg.at[0, :, mine], loc2.at[0]),
        pltpu.make_async_copy(w2u.at[me], pu.at[0, :, mine], loc2.at[1]),
        pltpu.make_async_copy(w2d.at[me], pd.at[0, mine, :], loc2.at[2]),
    )
    for c in w2_local:
        c.start()

    def r_wait(t, _):
        b = lax.rem(me + t, N)
        rcopy(rs.at[b], rr.at[b], rss.at[t], rrs.at[b], {"expert": b}).wait_recv()
        return 0

    lax.fori_loop(1, N, r_wait, 0)

    def combine(j, _):
        at = cols(j, 256)
        back = rr[...].reshape(N * MOST, width)
        over = (((0,), (0,)), ((), ()))
        total = lax.dot_general(whi[:, at], back, over, preferred_element_type=F32)
        total = total + lax.dot_general(wlo[:, at], back, over, preferred_element_type=F32)
        mixed[at, :] = total.astype(BF16)
        return 0

    lax.fori_loop(0, tokens // 256, combine, 0)

    for c in w2_local:
        c.wait()

    def w2_wait(t, _):
        i = lax.rem(me + t, N)
        for c in w2(me, t, i):
            c.wait_recv()
        return 0

    lax.fori_loop(1, N, w2_wait, 0)

    def sent(t, _):
        i = lax.rem(me + t, N)
        for c in w1(i, t, me):
            c.wait_send()
        for c in w2(i, t, me):
            c.wait_send()
        rcopy(cs.at[i], cr.at[me], css.at[t], crs.at[me], {"expert": i}).wait_send()
        rcopy(xs.at[i], xr.at[me], xss.at[t], xrs.at[me], {"expert": i}).wait_send()
        rcopy(rs.at[i], rr.at[me], rss.at[t], rrs.at[me], {"expert": i}).wait_send()
        return 0

    lax.fori_loop(1, N, sent, 0)
    for c in (to_c, *y1, *y2, to_z, h_z, h_ya, h_yb, h_c0, h_fa, h_c1, h_fb, h_c2, h_c3):
        c.wait_send()


def local(tokens, expert_ids, gates, gate_weight, up_weight, down_weight, partner, capacity):
    rows, width = tokens.shape
    ff = gate_weight.shape[2]
    me = lax.axis_index("expert")
    slots = jnp.arange(N, dtype=I32)
    mate = jnp.sum(jnp.where(slots == me, partner, 0))
    limit = jnp.sum(jnp.where(slots == mate, capacity, 0)).astype(F32)
    lim = jnp.broadcast_to(limit, (8, 128))
    piece = ff // N
    vmem = pl.BlockSpec(memory_space=pltpu.VMEM)
    smem = pl.BlockSpec(memory_space=pltpu.SMEM)
    anyw = pl.BlockSpec(memory_space=pl.ANY)
    V, D = pltpu.VMEM, pltpu.SemaphoreType.DMA
    return pl.pallas_call(
        kernel,
        out_shape=(
            jax.ShapeDtypeStruct((rows, width), BF16),
            jax.ShapeDtypeStruct(gate_weight.shape, BF16),
            jax.ShapeDtypeStruct(up_weight.shape, BF16),
            jax.ShapeDtypeStruct(down_weight.shape, BF16),
        ),
        in_specs=[vmem, vmem, vmem, smem, anyw, anyw, anyw, anyw],
        out_specs=(vmem, anyw, anyw, anyw),
        scratch_shapes=[
            V((rows, width), BF16), V((width, ff), BF16), V((width, ff), BF16), V((ff, width), BF16),
            V((N, rows), I32), V((N, rows), F32), V((N * MOST, rows), BF16), V((N * MOST, rows), BF16),
            V((N, MOST, width), BF16), V((N, MOST, width), BF16), V((N, 8, 128), F32), V((N, 8, 128), F32),
            V((N, 8, 128), F32), V((CAP, N * MOST), BF16), V((CAP, width), BF16),
            V((2, CAP, ff // 2), BF16), V((2, CAP, ff // 2), BF16), V((2, CAP, ff // 2), F32),
            V((2, 2, CAP, 256), BF16), V((2, 2, CAP, 256), BF16), V((2, CAP, 256), BF16), V((2, CAP, 256), BF16),
            V((2, CAP, 128), BF16), V((2, CAP, 128), BF16), V((CAP, ff), BF16), V((CAP, width), BF16),
            V((N, MOST, width), BF16), V((N, MOST, width), BF16),
            V((N, width, piece), BF16), V((N, width, piece), BF16), V((N, piece, width), BF16),
            V((N, width, piece), BF16), V((N, width, piece), BF16), V((N, piece, width), BF16),
            D((4,)), D((3,)), D((3,)), D((3, N)), D((3, N)), D((3, N)), D((3, N)),
            D((N,)), D((N,)), D((N,)), D((N,)), D((N,)), D((N,)), D((16,)), D((16,)),
        ],
        compiler_params=pltpu.CompilerParams(
            collective_id=0, has_side_effects=True, vmem_limit_bytes=67043328
        ),
        name="moe_swap",
    )(expert_ids.T, gates.T, lim, partner, tokens, gate_weight, up_weight, down_weight)


def solution(mesh):
    return jax.shard_map(
        local,
        mesh=mesh,
        in_specs=(
            P("expert", "dp"),
            P("expert", None),
            P("expert", None),
            P("expert", "dp", None),
            P("expert", "dp", None),
            P("expert", None, "dp"),
            P(),
            P(),
        ),
        out_specs=(
            P("expert", "dp"),
            P("expert", "dp", None),
            P("expert", "dp", None),
            P("expert", None, "dp"),
        ),
        check_vma=False,
    )
```

time: 665 us -> 433 us (0.65)
  the two profiles are of different devices: /device:TPU:57 before, /device:TPU:143 now
where the time goes in v1:
time: 433 us; the launch traced here: 432 us
  Pallas kernels  413 us (95%)
  local copies, waits for them, and re-layouts  14.9 us (3%)
    pallas_call x1, Pallas kernels, local(): pl.pallas_call(kernel, out_shape=(jax.ShapeDtypeStruct((rows, width), BF1...  413 us

profile of v1, /device:TPU:143, one launch (start us, length us, event | category | flops | bytes accessed | tf_op | source)
XLA Modules:
  0.0 432.4 jit_solution(9963023036426108362)
XLA Ops:
  0.6 0.0 copy-start.2
  0.6 1.4 fusion
  2.1 1.9 fusion.1
  4.7 0.6 broadcast_in_dim.9.lim
  5.3 2.2 copy.12.tok_h
  7.5 0.0 copy-done.2
  7.5 2.4 copy.13.wd_h
  9.9 412.8 %moe_swap.1 = (bf16[1024,448]{1,0:T(8,128)(2,1)}, bf16[1,448,2048]{2,1,0:T(8,128)(2,1)}, bf16[1,448,2048]{2,1,0:T(8,128)(2,1)}, bf16[1,2048,448]{2,1,0:T(8,128)(2,1)}) custom-call(s32[8,1024]{1,0:T(8,128)} %bitcast.2, f32[8,1024]{1,0:T(8,128)} %bitcast.3, f32[8,128]{1,0:T(8,128)} %broadcast_in_dim.9.lim, s32[16]{0:T(128)} %partner.1, ...), custom_call_target="tpu_custom_call" | custom-call | tf_op jit(solution)/shard_map/moe_swap/pallas_call | solution.py:409
  422.8 2.2 copy.14
  425.0 0.0 copy-start.1
  425.0 4.0 copy.15
  429.0 0.0 copy-done.1
  429.0 0.0 copy-start
  429.0 1.2 copy.18
  430.2 0.9 copy-done
  431.1 1.2 copy.19
Async XLA Ops:
  0.6 6.9 %copy-start.2 = (bf16[1,2048,448]{1,2,0:T(8,128)(2,1)S(1)}, bf16[1,2048,448]{1,2,0:T(8,128)(2,1)}, u32[]{:S(2)}) copy-start(bf16[1,2048,448]{1,2,0:T(8,128)(2,1)} %param.13) | copy-start | bytes 5505028
  425.0 4.0 copy-start.1
  429.0 2.2 copy-start

commit v2 on v1

--- a/solution.py
+++ b/solution.py
@@ -14,6 +14,9 @@
 F32 = jnp.float32
 BF16 = jnp.bfloat16
 I32 = jnp.int32
+LANES = (((1,), (1,)), ((), ()))
+ROWS = (((0,), (0,)), ((), ()))
+EARLY = 4
 
 
 def iota(shape, axis):
@@ -27,15 +30,15 @@
 
 
 def kernel(
-    ids, gates, lim, partner, tok_h, wg_h, wu_h, wd_h,
+    ids, gates, capacity, partner, tok_h, wg_h, wu_h, wd_h,
     mixed, pg, pu, pd,
     tok, wg, wu, wd, key, gat, whi, wlo,
     xs, xr, cs, cr, offs, pm, picked,
     cbs, cbr, acc, y1s, y1r, y2s, y2r, zs, zr, hid, eo, rs, rr,
-    w1g, w1u, w1d, w2g, w2u, w2d,
-    loc, loc1, loc2, w1ss, w1rs, w2ss, w2rs, xss, xrs, css, crs, rss, rrs, dss, drs,
+    w1b, w2b,
+    loc, w1ss, w1rs, w2ss, w2rs, xss, xrs, css, crs, rss, rrs, dss, drs,
 ):
-    tokens, width = tok_h.shape
+    width, tokens = tok_h.shape
     me = lax.axis_index("expert")
     dp = lax.axis_index("dp")
     yy, zl, cc = lax.div(dp, 4), lax.rem(lax.div(dp, 2), 2), lax.rem(dp, 2)
@@ -47,7 +50,8 @@
     yb = 3 - yy
     yc = lax.rem(yy + 2, 4)
     dev_c = {"dp": dp + 1 - 2 * cc}
-    dev_z = {"dp": dp + 2 - 4 * zl}
+    dpz = dp + 2 - 4 * zl
+    dev_z = {"dp": dpz}
     dev_ya = {"dp": at_y(ya)}
     dev_yb = {"dp": at_y(yb)}
 
@@ -66,37 +70,22 @@
         pl.semaphore_signal(barrier, inc=1, device_id={"expert": lax.rem(me + t, N)}, device_id_type=MESH)
         return 0
 
+    def hello_z(t, _):
+        dev = {"dp": dpz, "expert": lax.rem(me + t, N)}
+        pl.semaphore_signal(barrier, inc=1, device_id=dev, device_id_type=MESH)
+        return 0
+
     lax.fori_loop(1, N, hello, 0)
-    for d in (dev_c, dev_z, dev_ya, dev_yb):
+    lax.fori_loop(0, N, hello_z, 0)
+    for d in (dev_c, dev_ya, dev_yb):
         pl.semaphore_signal(barrier, inc=1, device_id=d, device_id_type=MESH)
-    pl.semaphore_wait(barrier, N - 1 + 4)
+    pl.semaphore_wait(barrier, 2 * N - 1 + 3)
+
+    def turn(t):
+        return lax.rem(me + 5 * t, N)
 
     def cols(i, n=128):
         return pl.ds(pl.multiple_of(i * n, n), n)
-
-    def w1(i, k, dst):
-        c = cols(i)
-        return (
-            rcopy(wg_h.at[0, :, c], w1g.at[dst], w1ss.at[0, k], w1rs.at[0, dst], {"expert": i}),
-            rcopy(wu_h.at[0, :, c], w1u.at[dst], w1ss.at[1, k], w1rs.at[1, dst], {"expert": i}),
-            rcopy(wd_h.at[0, c, :], w1d.at[dst], w1ss.at[2, k], w1rs.at[2, dst], {"expert": i}),
-        )
-
-    def w1_send(t, _):
-        i = lax.rem(me + t, N)
-        for c in w1(i, t, me):
-            c.start()
-        return 0
-
-    lax.fori_loop(1, N, w1_send, 0)
-    mine = cols(me)
-    w1_local = (
-        pltpu.make_async_copy(wg_h.at[0, :, mine], w1g.at[me], loc1.at[0]),
-        pltpu.make_async_copy(wu_h.at[0, :, mine], w1u.at[me], loc1.at[1]),
-        pltpu.make_async_copy(wd_h.at[0, mine, :], w1d.at[me], loc1.at[2]),
-    )
-    for c in w1_local:
-        c.start()
 
     e_of = iota((N, tokens), 0)
     named = jnp.zeros((N, tokens), I32)
@@ -118,10 +107,10 @@
     row_of = iota((MOST, tokens), 0)
 
     def dispatch(t, _):
-        e = lax.rem(me + t, N)
+        e = turn(t)
         krow = key[pl.ds(e, 1), :]
         pick = (row_of == krow).astype(F32).astype(BF16)
-        rows = jnp.dot(pick, tok[...], preferred_element_type=F32).astype(BF16)
+        rows = lax.dot_general(pick, tok[...], LANES, preferred_element_type=F32).astype(BF16)
         total = jnp.sum(jnp.where(krow >= 0, 1.0, 0.0), axis=1, keepdims=True)
         total = jnp.broadcast_to(total, (8, 128))
 
@@ -140,6 +129,19 @@
         return 0
 
     lax.fori_loop(0, N, dispatch, 0)
+
+    def w1(i, t, src):
+        return [
+            rcopy(ref.at[0, :, cols(i)], w1b.at[n, src], w1ss.at[n, t], w1rs.at[n, src], {"dp": dpz, "expert": i})
+            for n, ref in enumerate((wg_h, wu_h, wd_h))
+        ]
+
+    def w1_send(t, _):
+        for c in w1(turn(t), t, me):
+            c.start()
+        return 0
+
+    lax.fori_loop(0, N, w1_send, 0)
 
     def spread(e, _):
         krow = key[pl.ds(e, 1), :]
@@ -153,14 +155,14 @@
     lax.fori_loop(0, N, spread, 0)
 
     def x_wait(t, _):
-        b = lax.rem(me + t, N)
+        b = turn(t)
         rcopy(cs.at[b], cr.at[b], css.at[t], crs.at[b], {"expert": b}).wait_recv()
         rcopy(xs.at[b], xr.at[b], xss.at[t], xrs.at[b], {"expert": b}).wait_recv()
         return 0
 
     lax.fori_loop(1, N, x_wait, 0)
 
-    limit = lim[0:1, 0:1]
+    limit = capacity[partner[me]].astype(F32)
     p_of = iota((CAP, 2 * MOST), 0).astype(F32)
     l_of = iota((CAP, 2 * MOST), 1)
     i_of = lax.rem(l_of, MOST).astype(F32)
@@ -187,9 +189,7 @@
     def theirs(j, _):
         for w, ref in enumerate((wg, wu)):
             at = pl.ds(pl.multiple_of((1 - cc) * half + j * 256, 256), 256)
-            cbs[w, :, cols(j, 256)] = jnp.dot(
-                picked[...], ref[:, at], preferred_element_type=F32
-            ).astype(BF16)
+            cbs[w, :, cols(j, 256)] = jnp.dot(picked[...], ref[:, at], preferred_element_type=F32)
         return 0
 
     def ours(j, _):
@@ -206,7 +206,7 @@
 
     def block(w, q):
         at = cols(q, 256)
-        return acc[w, :, at] + cbr[w, :, at].astype(F32)
+        return acc[w, :, at] + cbr[w, :, at]
 
     y1 = []
     for w, (q, dev) in enumerate(((ya, dev_ya), (yb, dev_yb))):
@@ -260,6 +260,29 @@
     h_yb.start()
     h_c0 = to((everyrow, me_q), 9, dev_c)
     h_c0.start()
+    def w1_wait(t, _):
+        for c in w1(me, t, turn(t)):
+            c.wait_recv()
+        return 0
+
+    def w2(k, t, src):
+        return [
+            rcopy(w2b.at[n, k], ref.at[0, :, cols(src)], w2ss.at[n, t], w2rs.at[n, src], {"dp": dpz, "expert": k})
+            for n, ref in enumerate((pg, pu, pd))
+        ]
+
+    def w2_send(t, _):
+        k = turn(t)
+        s = partner[k]
+        for n in range(3):
+            w2b[n, k] = w1b[n, s]
+        for c in w2(k, t, me):
+            c.start()
+        return 0
+
+    lax.fori_loop(0, N, w1_wait, 0)
+    lax.fori_loop(0, EARLY, w2_send, 0)
+
     to((everyrow, chunk(cc, ya)), 7, dev_ya).wait_recv()
     h_fa = to((top, chunk(cc, ya)), 10, dev_yb)
     h_fa.start()
@@ -280,13 +303,13 @@
     to((everyrow, chunk(1 - cc, yc)), 14, dev_c).wait_recv()
 
     loads[3].wait()
-    eo[...] = jnp.dot(hid[...], wd[...], preferred_element_type=F32).astype(BF16)
+    eo[...] = lax.dot_general(hid[...], wd[...], LANES, preferred_element_type=F32).astype(BF16)
 
     i_row = iota((MOST, CAP), 0).astype(F32)
     p_lane = iota((MOST, CAP), 1).astype(F32)
 
     def reply(t, _):
-        b = lax.rem(me + t, N)
+        b = turn(t)
         count, start = cr[b][0:1, 0:1], offs[b][0:1, 0:1]
         hit = (p_lane == start + i_row) & (i_row < count) & (p_lane < limit)
         rows = jnp.dot(
@@ -306,50 +329,10 @@
 
     lax.fori_loop(0, N, reply, 0)
 
-    for c in w1_local:
-        c.wait()
-
-    def w1_wait(t, _):
-        s = lax.rem(me + t, N)
-        for c in w1(me, t, s):
-            c.wait_recv()
-        return 0
-
-    lax.fori_loop(1, N, w1_wait, 0)
-
-    def w2(k, t, i):
-        c = cols(i)
-        return (
-            rcopy(w2g.at[k], pg.at[0, :, c], w2ss.at[0, t], w2rs.at[0, i], {"expert": k}),
-            rcopy(w2u.at[k], pu.at[0, :, c], w2ss.at[1, t], w2rs.at[1, i], {"expert": k}),
-            rcopy(w2d.at[k], pd.at[0, c, :], w2ss.at[2, t], w2rs.at[2, i], {"expert": k}),
-        )
-
-    def w2_send(t, _):
-        k = lax.rem(me + t, N)
-        s = partner[k]
-        w2g[k] = w1g[s]
-        w2u[k] = w1u[s]
-        w2d[k] = w1d[s]
-
-        @pl.when(t > 0)
-        def _():
-            for c in w2(k, t, me):
-                c.start()
-
-        return 0
-
-    lax.fori_loop(0, N, w2_send, 0)
-    w2_local = (
-        pltpu.make_async_copy(w2g.at[me], pg.at[0, :, mine], loc2.at[0]),
-        pltpu.make_async_copy(w2u.at[me], pu.at[0, :, mine], loc2.at[1]),
-        pltpu.make_async_copy(w2d.at[me], pd.at[0, mine, :], loc2.at[2]),
-    )
-    for c in w2_local:
-        c.start()
+    lax.fori_loop(EARLY, N, w2_send, 0)
 
     def r_wait(t, _):
-        b = lax.rem(me + t, N)
+        b = turn(t)
         rcopy(rs.at[b], rr.at[b], rss.at[t], rrs.at[b], {"expert": b}).wait_recv()
         return 0
 
@@ -358,31 +341,31 @@
     def combine(j, _):
         at = cols(j, 256)
         back = rr[...].reshape(N * MOST, width)
-        over = (((0,), (0,)), ((), ()))
-        total = lax.dot_general(whi[:, at], back, over, preferred_element_type=F32)
-        total = total + lax.dot_general(wlo[:, at], back, over, preferred_element_type=F32)
-        mixed[at, :] = total.astype(BF16)
+        total = lax.dot_general(back, whi[:, at], ROWS, preferred_element_type=F32)
+        total = total + lax.dot_general(back, wlo[:, at], ROWS, preferred_element_type=F32)
+        mixed[:, at] = total.astype(BF16)
         return 0
 
     lax.fori_loop(0, tokens // 256, combine, 0)
 
-    for c in w2_local:
-        c.wait()
-
     def w2_wait(t, _):
-        i = lax.rem(me + t, N)
-        for c in w2(me, t, i):
+        for c in w2(me, t, turn(t)):
             c.wait_recv()
         return 0
 
-    lax.fori_loop(1, N, w2_wait, 0)
+    lax.fori_loop(0, N, w2_wait, 0)
+
+    def w_sent(t, _):
+        for c in w1(turn(t), t, me):
+            c.wait_send()
+        for c in w2(turn(t), t, me):
+            c.wait_send()
+        return 0
+
+    lax.fori_loop(0, N, w_sent, 0)
 
     def sent(t, _):
-        i = lax.rem(me + t, N)
-        for c in w1(i, t, me):
-            c.wait_send()
-        for c in w2(i, t, me):
-            c.wait_send()
+        i = turn(t)
         rcopy(cs.at[i], cr.at[me], css.at[t], crs.at[me], {"expert": i}).wait_send()
         rcopy(xs.at[i], xr.at[me], xss.at[t], xrs.at[me], {"expert": i}).wait_send()
         rcopy(rs.at[i], rr.at[me], rss.at[t], rrs.at[me], {"expert": i}).wait_send()
@@ -396,45 +379,39 @@
 def local(tokens, expert_ids, gates, gate_weight, up_weight, down_weight, partner, capacity):
     rows, width = tokens.shape
     ff = gate_weight.shape[2]
-    me = lax.axis_index("expert")
-    slots = jnp.arange(N, dtype=I32)
-    mate = jnp.sum(jnp.where(slots == me, partner, 0))
-    limit = jnp.sum(jnp.where(slots == mate, capacity, 0)).astype(F32)
-    lim = jnp.broadcast_to(limit, (8, 128))
-    piece = ff // N
     vmem = pl.BlockSpec(memory_space=pltpu.VMEM)
     smem = pl.BlockSpec(memory_space=pltpu.SMEM)
     anyw = pl.BlockSpec(memory_space=pl.ANY)
     V, D = pltpu.VMEM, pltpu.SemaphoreType.DMA
-    return pl.pallas_call(
+    mix, new_gate, new_up, new_down = pl.pallas_call(
         kernel,
         out_shape=(
-            jax.ShapeDtypeStruct((rows, width), BF16),
+            jax.ShapeDtypeStruct((width, rows), BF16),
             jax.ShapeDtypeStruct(gate_weight.shape, BF16),
             jax.ShapeDtypeStruct(up_weight.shape, BF16),
-            jax.ShapeDtypeStruct(down_weight.shape, BF16),
+            jax.ShapeDtypeStruct(gate_weight.shape, BF16),
         ),
-        in_specs=[vmem, vmem, vmem, smem, anyw, anyw, anyw, anyw],
+        in_specs=[vmem, vmem, smem, smem, anyw, anyw, anyw, anyw],
         out_specs=(vmem, anyw, anyw, anyw),
         scratch_shapes=[
-            V((rows, width), BF16), V((width, ff), BF16), V((width, ff), BF16), V((ff, width), BF16),
+            V((width, rows), BF16), V((width, ff), BF16), V((width, ff), BF16), V((width, ff), BF16),
             V((N, rows), I32), V((N, rows), F32), V((N * MOST, rows), BF16), V((N * MOST, rows), BF16),
             V((N, MOST, width), BF16), V((N, MOST, width), BF16), V((N, 8, 128), F32), V((N, 8, 128), F32),
             V((N, 8, 128), F32), V((CAP, N * MOST), BF16), V((CAP, width), BF16),
-            V((2, CAP, ff // 2), BF16), V((2, CAP, ff // 2), BF16), V((2, CAP, ff // 2), F32),
+            V((2, CAP, ff // 2), F32), V((2, CAP, ff // 2), F32), V((2, CAP, ff // 2), F32),
             V((2, 2, CAP, 256), BF16), V((2, 2, CAP, 256), BF16), V((2, CAP, 256), BF16), V((2, CAP, 256), BF16),
             V((2, CAP, 128), BF16), V((2, CAP, 128), BF16), V((CAP, ff), BF16), V((CAP, width), BF16),
             V((N, MOST, width), BF16), V((N, MOST, width), BF16),
-            V((N, width, piece), BF16), V((N, width, piece), BF16), V((N, piece, width), BF16),
-            V((N, width, piece), BF16), V((N, width, piece), BF16), V((N, piece, width), BF16),
-            D((4,)), D((3,)), D((3,)), D((3, N)), D((3, N)), D((3, N)), D((3, N)),
+            V((3, N, width, ff // N), BF16), V((3, N, width, ff // N), BF16),
+            D((4,)), D((3, N)), D((3, N)), D((3, N)), D((3, N)),
             D((N,)), D((N,)), D((N,)), D((N,)), D((N,)), D((N,)), D((16,)), D((16,)),
         ],
         compiler_params=pltpu.CompilerParams(
             collective_id=0, has_side_effects=True, vmem_limit_bytes=67043328
         ),
         name="moe_swap",
-    )(expert_ids.T, gates.T, lim, partner, tokens, gate_weight, up_weight, down_weight)
+    )(expert_ids.T, gates.T, capacity, partner, tokens.T, gate_weight, up_weight, down_weight.transpose(0, 2, 1))
+    return mix.T, new_gate, new_up, new_down.transpose(0, 2, 1)
 
 
 def solution(mesh):

time: 433 us -> 348 us (0.80)
  the two profiles are of different devices: /device:TPU:143 before, /device:TPU:57 now
where the time goes in v2:
time: 348 us; the launch traced here: 344 us
  Pallas kernels  336 us (97%)
  local copies, waits for them, and re-layouts  7.85 us (2%)
    pallas_call x1, Pallas kernels, local(): pl.pallas_call(kernel, out_shape=(jax.ShapeDtypeStruct((width, rows), BF1...  336 us
    unnamed x10, local copies, waits for them, and re-layouts  7.85 us

profile of v2, /device:TPU:57, one launch (start us, length us, event | category | flops | bytes accessed | tf_op | source)
XLA Modules:
  0.0 344.3 jit_solution(8736549827137852108)
XLA Ops:
  0.6 335.8 %moe_swap.1 = (bf16[448,1024]{1,0:T(8,128)(2,1)}, bf16[1,448,2048]{2,1,0:T(8,128)(2,1)}, bf16[1,448,2048]{2,1,0:T(8,128)(2,1)}, bf16[1,448,2048]{2,1,0:T(8,128)(2,1)}) custom-call(s32[8,1024]{1,0:T(8,128)} %bitcast.10, f32[8,1024]{1,0:T(8,128)} %bitcast.11, s32[16]{0:T(128)} %capacity.1, s32[16]{0:T(128)} %partner.1, bf16[448,1024]{1,0:T(8,128)(2,1)} %bitcast.9, ...), custom_call_target="tpu_custom_call" | custom-call | tf_op jit(solution)/shard_map/moe_swap/pallas_call | solution.py:386
  336.4 0.0 copy-start.2
  336.5 2.3 copy.16
  338.7 0.0 copy-done.2
  338.8 0.0 copy-start.1
  338.8 1.2 copy.17
  340.0 0.9 copy-done.1
  340.9 0.0 copy-start
  340.9 1.2 copy.18
  342.1 0.9 copy-done
  343.1 1.2 copy.19
Async XLA Ops:
  336.4 2.3 copy-start.2
  338.8 2.2 copy-start.1
  340.9 2.2 copy-start

commit v3 on v2

--- a/solution.py
+++ b/solution.py
@@ -17,6 +17,8 @@
 LANES = (((1,), (1,)), ((), ()))
 ROWS = (((0,), (0,)), ((), ()))
 EARLY = 4
+SWAP_REFS = {True: 6, False: 13}
+PLANS = ((1, 1), None)
 
 
 def iota(shape, axis):
@@ -29,15 +31,238 @@
     )
 
 
-def kernel(
-    ids, gates, capacity, partner, tok_h, wg_h, wu_h, wd_h,
-    mixed, pg, pu, pd,
-    tok, wg, wu, wd, key, gat, whi, wlo,
-    xs, xr, cs, cr, offs, pm, picked,
-    cbs, cbr, acc, y1s, y1r, y2s, y2r, zs, zr, hid, eo, rs, rr,
-    w1b, w2b,
-    loc, w1ss, w1rs, w2ss, w2rs, xss, xrs, css, crs, rss, rrs, dss, drs,
+def spread_swap(me, dpz, cols, turn, partner, weights, placed, w1b, w2b, w1ss, w1rs, w2ss, w2rs):
+    def w1(i, t, src):
+        return [
+            rcopy(ref.at[0, :, cols(i)], w1b.at[n, src], w1ss.at[n, t], w1rs.at[n, src], {"dp": dpz, "expert": i})
+            for n, ref in enumerate(weights)
+        ]
+
+    def w2(k, t, src):
+        return [
+            rcopy(w2b.at[n, k], ref.at[0, :, cols(src)], w2ss.at[n, t], w2rs.at[n, src], {"dp": dpz, "expert": k})
+            for n, ref in enumerate(placed)
+        ]
+
+    def w1_send(t, _):
+        for c in w1(turn(t), t, me):
+            c.start()
+        return 0
+
+    def w1_wait(t, _):
+        for c in w1(me, t, turn(t)):
+            c.wait_recv()
+        return 0
+
+    def w2_send(t, _):
+        k = turn(t)
+        s = partner[k]
+        for n in range(3):
+            w2b[n, k] = w1b[n, s]
+        for c in w2(k, t, me):
+            c.start()
+        return 0
+
+    def w2_wait(t, _):
+        for c in w2(me, t, turn(t)):
+            c.wait_recv()
+        return 0
+
+    def w_sent(t, _):
+        for c in w1(turn(t), t, me) + w2(turn(t), t, me):
+            c.wait_send()
+        return 0
+
+    def swap(point):
+        if point == 1:
+            lax.fori_loop(0, N, w1_send, 0)
+        if point == 6:
+            lax.fori_loop(0, N, w1_wait, 0)
+            lax.fori_loop(0, EARLY, w2_send, 0)
+        if point == 8:
+            lax.fori_loop(EARLY, N, w2_send, 0)
+        if point == 9:
+            lax.fori_loop(0, N, w2_wait, 0)
+            lax.fori_loop(0, N, w_sent, 0)
+
+    return swap
+
+
+def row_swap(
+    plan, me, partner, weights, placed, q0, q1, q2, e0, e1, e2, zsend, relay, xsend, xrelay, local_sem, ss, rs
 ):
+    near, far = plan
+    row_box, far_box = (q0, q1, q2), (e0, e1, e2)
+    r, x = lax.div(me, 4), lax.rem(me, 4)
+    rp, rm = lax.rem(r + 1, 4), lax.rem(r + 3, 4)
+    xp, xm, xo = lax.rem(x + 1, 4), lax.rem(x + 3, 4), lax.rem(x + 2, 4)
+    quarter = q0.shape[2]
+    left, right = pl.ds(0, quarter // 2), pl.ds(quarter // 2, quarter // 2)
+    opposite = 2 * near
+
+    def at(row, col):
+        return {"expert": row * 4 + col}
+
+    def part(ref, j):
+        return ref.at[0, :, pl.ds(pl.multiple_of(j * quarter, quarter), quarter)]
+
+    def row_at(i):
+        return lax.div(partner[i], 4)
+
+    def find(target, k):
+        seen, found = 0, 0
+        for i in range(4):
+            hit = row_at(r * 4 + i) == target
+            found = jnp.where(hit & (seen == k), i, found)
+            seen = seen + jnp.where(hit, 1, 0)
+        return found
+
+    def held(col):
+        s = partner[r * 4 + col]
+        sr, si = lax.div(s, 4), lax.rem(s, 4)
+        order = 0
+        for i in range(4):
+            order = order + jnp.where((si > i) & (row_at(sr * 4 + i) == r), 1, 0)
+        d = lax.rem(sr - r + 4, 4)
+        place = jnp.where(d == 3, order, jnp.where(d == 1, near + order, opposite + order))
+        return d == 0, si, jnp.minimum(place, e0.shape[0] - 1)
+
+    def x1(n, sender=False):
+        ways = ((xp, xm), (xm, xp), (xo, xo))
+        return [
+            rcopy(part(weights[n], to), row_box[n].at[x if sender else src], ss.at[n, d], rs.at[n, d], at(r, to))
+            for d, (to, src) in enumerate(ways)
+        ]
+
+    def x1_local(n):
+        return pltpu.make_async_copy(part(weights[n], x), row_box[n].at[x], local_sem.at[n])
+
+    def z1(n, group):
+        out = []
+        if group:
+            for k in range(near):
+                out.append((zsend.at[n, k], far_box[n].at[k], rp))
+                out.append((zsend.at[n, near + k], far_box[n].at[near + k], rm))
+        else:
+            for k in range(far):
+                out.append((zsend.at[n, 2 * near + k, :, left], relay.at[n, 0, k], rp))
+                out.append((zsend.at[n, 2 * near + k, :, right], relay.at[n, 1, k], rm))
+        first = 3 + 2 * far * group
+        return [
+            rcopy(a, b, ss.at[n, first + i], rs.at[n, first + i], at(row, x)) for i, (a, b, row) in enumerate(out)
+        ]
+
+    def z2(n):
+        out = []
+        for k in range(far):
+            for w, (cut, row) in enumerate(((left, rp), (right, rm))):
+                i = 16 + 2 * k + w
+                out.append(
+                    rcopy(relay.at[n, w, k], far_box[n].at[opposite + k, :, cut], ss.at[n, i], rs.at[n, i], at(row, x))
+                )
+        return out
+
+    def x2(n, sender=False):
+        return [
+            rcopy(xsend.at[n, 1], part(placed[n], x if sender else xm), ss.at[n, 26], rs.at[n, 26], at(r, xp)),
+            rcopy(xsend.at[n, 2], part(placed[n], x if sender else xp), ss.at[n, 27], rs.at[n, 27], at(r, xm)),
+        ]
+
+    def x2_first(n):
+        return rcopy(xsend.at[n, 3], xrelay.at[n], ss.at[n, 28], rs.at[n, 28], at(r, xm))
+
+    def x2_last(n, sender=False):
+        return rcopy(
+            xrelay.at[n], part(placed[n], xp if sender else xo), ss.at[n, 29], rs.at[n, 29], at(r, xm)
+        )
+
+    def x2_local(n):
+        return pltpu.make_async_copy(xsend.at[n, 0], part(placed[n], x), local_sem.at[3 + n])
+
+    def x1_send(n):
+        for c in x1(n, True):
+            c.start()
+        x1_local(n).start()
+
+    def z1_send(n):
+        for c in x1(n):
+            c.wait_recv()
+        x1_local(n).wait()
+        for k in range(far):
+            zsend[n, 2 * near + k] = row_box[n][find(lax.rem(r + 2, 4), k)]
+        for k in range(near):
+            zsend[n, k] = row_box[n][find(rp, k)]
+            zsend[n, near + k] = row_box[n][find(rm, k)]
+        for c in z1(n, 0) + z1(n, 1):
+            c.start()
+
+    def z2_send(n):
+        for c in z1(n, 0):
+            c.wait_recv()
+        for c in z2(n):
+            c.start()
+
+    def x2_send(n):
+        for c in z1(n, 1) + z2(n):
+            c.wait_recv()
+        for j, col in enumerate((x, xp, xm, xo)):
+            stays, si, place = held(col)
+            xsend[n, j] = jnp.where(stays, row_box[n][si], far_box[n][place])
+        for c in [x2_first(n)] + x2(n, True):
+            c.start()
+        x2_local(n).start()
+
+    def x2_relay(n):
+        x2_first(n).wait_recv()
+        x2_last(n, True).start()
+
+    def finish(n):
+        for c in x2(n):
+            c.wait_recv()
+        x2_last(n).wait_recv()
+        x2_local(n).wait()
+        for c in x1(n, True) + z1(n, 0) + z1(n, 1) + z2(n) + x2(n, True) + [x2_first(n), x2_last(n, True)]:
+            c.wait_send()
+
+    def swap(point):
+        if point == 0:
+            x1_send(0)
+        if point == 1:
+            x1_send(1)
+            x1_send(2)
+        if point == 2:
+            z1_send(0)
+        if point == 3:
+            z1_send(1)
+        if point == 6:
+            z2_send(0)
+            z1_send(2)
+            z2_send(1)
+        if point == 8:
+            x2_send(0)
+            z2_send(2)
+            x2_send(1)
+            x2_relay(0)
+        if point == 9:
+            x2_send(2)
+            for n in range(1, 3):
+                x2_relay(n)
+            for n in range(3):
+                finish(n)
+
+    return swap
+
+
+def kernel(plan, *refs):
+    (
+        ids, gates, capacity, partner, tok_h, wg_h, wu_h, wd_h,
+        mixed, pg, pu, pd,
+        tok, wg, wu, wd, key, gat, whi, wlo,
+        xs, xr, cs, cr, offs, pm, picked,
+        cbs, cbr, acc, y1s, y1r, y2s, y2r, zs, zr, hid, eo, rs, rr,
+        loc, xss, xrs, css, crs, rss, rrs, dss, drs,
+    ) = refs[: len(refs) - SWAP_REFS[plan is None]]
+    swap_refs = refs[len(refs) - SWAP_REFS[plan is None] :]
     width, tokens = tok_h.shape
     me = lax.axis_index("expert")
     dp = lax.axis_index("dp")
@@ -76,16 +301,24 @@
         return 0
 
     lax.fori_loop(1, N, hello, 0)
-    lax.fori_loop(0, N, hello_z, 0)
+    other = N if plan is None else 1
+    lax.fori_loop(0, other, hello_z, 0)
     for d in (dev_c, dev_ya, dev_yb):
         pl.semaphore_signal(barrier, inc=1, device_id=d, device_id_type=MESH)
-    pl.semaphore_wait(barrier, 2 * N - 1 + 3)
+    pl.semaphore_wait(barrier, N - 1 + other + 3)
 
     def turn(t):
         return lax.rem(me + 5 * t, N)
 
     def cols(i, n=128):
         return pl.ds(pl.multiple_of(i * n, n), n)
+
+    weights, placed = (wg_h, wu_h, wd_h), (pg, pu, pd)
+    if plan is None:
+        swap = spread_swap(me, dpz, cols, turn, partner, weights, placed, *swap_refs)
+    else:
+        swap = row_swap(plan, me, partner, weights, placed, *swap_refs)
+    swap(0)
 
     e_of = iota((N, tokens), 0)
     named = jnp.zeros((N, tokens), I32)
@@ -130,18 +363,7 @@
 
     lax.fori_loop(0, N, dispatch, 0)
 
-    def w1(i, t, src):
-        return [
-            rcopy(ref.at[0, :, cols(i)], w1b.at[n, src], w1ss.at[n, t], w1rs.at[n, src], {"dp": dpz, "expert": i})
-            for n, ref in enumerate((wg_h, wu_h, wd_h))
-        ]
-
-    def w1_send(t, _):
-        for c in w1(turn(t), t, me):
-            c.start()
-        return 0
-
-    lax.fori_loop(0, N, w1_send, 0)
+    swap(1)
 
     def spread(e, _):
         krow = key[pl.ds(e, 1), :]
@@ -153,6 +375,8 @@
         return 0
 
     lax.fori_loop(0, N, spread, 0)
+
+    swap(2)
 
     def x_wait(t, _):
         b = turn(t)
@@ -201,6 +425,7 @@
     lax.fori_loop(0, half // 256, theirs, 0)
     to_c = rcopy(cbs, cbr, dss.at[0], drs.at[0], dev_c)
     to_c.start()
+    swap(3)
     lax.fori_loop(0, half // 256, ours, 0)
     to_c.wait_recv()
 
@@ -215,6 +440,7 @@
         c = rcopy(y1s.at[w], y1r.at[w], dss.at[1 + w], drs.at[1 + w], dev)
         c.start()
         y1.append(c)
+    swap(4)
     y2 = []
     for w, (q, dev) in enumerate(((yb, dev_yb), (ya, dev_ya))):
         y1[w].wait_recv()
@@ -222,6 +448,7 @@
         c = rcopy(y2s.at[w], y2r.at[w], dss.at[3 + w], drs.at[3 + w], dev)
         c.start()
         y2.append(c)
+    swap(5)
     for w in range(2):
         acc[w, :, cols(yy, 256)] = block(w, yy) + y1r[w, 0].astype(F32)
     for w in range(2):
@@ -260,29 +487,7 @@
     h_yb.start()
     h_c0 = to((everyrow, me_q), 9, dev_c)
     h_c0.start()
-    def w1_wait(t, _):
-        for c in w1(me, t, turn(t)):
-            c.wait_recv()
-        return 0
-
-    def w2(k, t, src):
-        return [
-            rcopy(w2b.at[n, k], ref.at[0, :, cols(src)], w2ss.at[n, t], w2rs.at[n, src], {"dp": dpz, "expert": k})
-            for n, ref in enumerate((pg, pu, pd))
-        ]
-
-    def w2_send(t, _):
-        k = turn(t)
-        s = partner[k]
-        for n in range(3):
-            w2b[n, k] = w1b[n, s]
-        for c in w2(k, t, me):
-            c.start()
-        return 0
-
-    lax.fori_loop(0, N, w1_wait, 0)
-    lax.fori_loop(0, EARLY, w2_send, 0)
-
+    swap(6)
     to((everyrow, chunk(cc, ya)), 7, dev_ya).wait_recv()
     h_fa = to((top, chunk(cc, ya)), 10, dev_yb)
     h_fa.start()
@@ -303,6 +508,7 @@
     to((everyrow, chunk(1 - cc, yc)), 14, dev_c).wait_recv()
 
     loads[3].wait()
+    swap(7)
     eo[...] = lax.dot_general(hid[...], wd[...], LANES, preferred_element_type=F32).astype(BF16)
 
     i_row = iota((MOST, CAP), 0).astype(F32)
@@ -329,7 +535,7 @@
 
     lax.fori_loop(0, N, reply, 0)
 
-    lax.fori_loop(EARLY, N, w2_send, 0)
+    swap(8)
 
     def r_wait(t, _):
         b = turn(t)
@@ -348,21 +554,7 @@
 
     lax.fori_loop(0, tokens // 256, combine, 0)
 
-    def w2_wait(t, _):
-        for c in w2(me, t, turn(t)):
-            c.wait_recv()
-        return 0
-
-    lax.fori_loop(0, N, w2_wait, 0)
-
-    def w_sent(t, _):
-        for c in w1(turn(t), t, me):
-            c.wait_send()
-        for c in w2(turn(t), t, me):
-            c.wait_send()
-        return 0
-
-    lax.fori_loop(0, N, w_sent, 0)
+    swap(9)
 
     def sent(t, _):
         i = turn(t)
@@ -376,20 +568,30 @@
         c.wait_send()
 
 
-def local(tokens, expert_ids, gates, gate_weight, up_weight, down_weight, partner, capacity):
-    rows, width = tokens.shape
-    ff = gate_weight.shape[2]
+def layer(plan, rows, width, ff, *args):
     vmem = pl.BlockSpec(memory_space=pltpu.VMEM)
     smem = pl.BlockSpec(memory_space=pltpu.SMEM)
     anyw = pl.BlockSpec(memory_space=pl.ANY)
     V, D = pltpu.VMEM, pltpu.SemaphoreType.DMA
-    mix, new_gate, new_up, new_down = pl.pallas_call(
-        kernel,
+    quarter = ff // 4
+    if plan is None:
+        swap_scratch = [V((3, N, width, ff // N), BF16)] * 2 + [D((3, N))] * 4
+    else:
+        near, far = plan
+        half = max(far, 1)
+        swap_scratch = [
+            *[V((4, width, quarter), BF16)] * 3, *[V((2 * near + far, width, quarter), BF16)] * 3,
+            V((3, 2 * near + far, width, quarter), BF16),
+            V((3, 2, half, width, quarter // 2), BF16), V((3, 4, width, quarter), BF16), V((3, width, quarter), BF16),
+            D((6,)), D((3, 32)), D((3, 32)),
+        ]
+    return pl.pallas_call(
+        functools.partial(kernel, plan),
         out_shape=(
             jax.ShapeDtypeStruct((width, rows), BF16),
-            jax.ShapeDtypeStruct(gate_weight.shape, BF16),
-            jax.ShapeDtypeStruct(up_weight.shape, BF16),
-            jax.ShapeDtypeStruct(gate_weight.shape, BF16),
+            jax.ShapeDtypeStruct((1, width, ff), BF16),
+            jax.ShapeDtypeStruct((1, width, ff), BF16),
+            jax.ShapeDtypeStruct((1, width, ff), BF16),
         ),
         in_specs=[vmem, vmem, smem, smem, anyw, anyw, anyw, anyw],
         out_specs=(vmem, anyw, anyw, anyw),
@@ -402,15 +604,34 @@
             V((2, 2, CAP, 256), BF16), V((2, 2, CAP, 256), BF16), V((2, CAP, 256), BF16), V((2, CAP, 256), BF16),
             V((2, CAP, 128), BF16), V((2, CAP, 128), BF16), V((CAP, ff), BF16), V((CAP, width), BF16),
             V((N, MOST, width), BF16), V((N, MOST, width), BF16),
-            V((3, N, width, ff // N), BF16), V((3, N, width, ff // N), BF16),
-            D((4,)), D((3, N)), D((3, N)), D((3, N)), D((3, N)),
+            D((4,)),
             D((N,)), D((N,)), D((N,)), D((N,)), D((N,)), D((N,)), D((16,)), D((16,)),
-        ],
+        ]
+        + swap_scratch,
         compiler_params=pltpu.CompilerParams(
-            collective_id=0, has_side_effects=True, vmem_limit_bytes=67043328
+            collective_id=PLANS.index(plan), has_side_effects=True, vmem_limit_bytes=67043328
         ),
-        name="moe_swap",
-    )(expert_ids.T, gates.T, capacity, partner, tokens.T, gate_weight, up_weight, down_weight.transpose(0, 2, 1))
+        name="moe_swap_" + ("any" if plan is None else "%d%d" % plan),
+    )(*args)
+
+
+def local(tokens, expert_ids, gates, gate_weight, up_weight, down_weight, partner, capacity):
+    rows, width = tokens.shape
+    ff = gate_weight.shape[2]
+    slots = jnp.arange(N, dtype=I32)
+    ahead = jnp.remainder(partner // 4 - slots // 4, 4).reshape(4, 4)
+    near = jnp.max(jnp.sum((ahead == 1).astype(I32), axis=1))
+    far = jnp.max(jnp.sum((ahead == 2).astype(I32), axis=1))
+    choice = jnp.int32(len(PLANS) - 1)
+    for i, plan in reversed(list(enumerate(PLANS[:-1]))):
+        choice = jnp.where((near <= plan[0]) & (far <= plan[1]), i, choice)
+    args = (
+        expert_ids.T, gates.T, capacity, partner, tokens.T,
+        gate_weight, up_weight, down_weight.transpose(0, 2, 1),
+    )
+    mix, new_gate, new_up, new_down = lax.switch(
+        choice, [functools.partial(layer, plan, rows, width, ff) for plan in PLANS], *args
+    )
     return mix.T, new_gate, new_up, new_down.transpose(0, 2, 1)
 
 

time: 348 us -> 353 us (1.014)
  Pallas kernels: 336 us -> 340 us
    pallas_call x1, Pallas kernels: 336 us -> 340 us  [layer(): pl.pallas_call(functools.partial(kernel, plan), out_shape=(jax.ShapeDtype...]
where the time goes in v3:
time: 353 us; the launch traced here: 352 us
  Pallas kernels  340 us (96%)
  local copies, waits for them, and re-layouts  8.01 us (2%)
    pallas_call x1, Pallas kernels, layer(): pl.pallas_call(functools.partial(kernel, plan), out_shape=(jax.ShapeDtype...  340 us
    unnamed x10, local copies, waits for them, and re-layouts  7.85 us

profile of v3, /device:TPU:57, one launch (start us, length us, event | category | flops | bytes accessed | tf_op | source)
XLA Modules:
  0.0 352.3 jit_solution(7708156747916509081)
XLA Ops:
  0.6 0.7 compare_convert_fusion
  1.3 0.1 reshape.17
  1.4 0.1 reduce_sum.18
  1.5 0.6 reduce_max.18
  2.8 0.1 reshape.18
  2.9 0.1 reduce_sum.19
  3.0 0.6 reduce_max.19
  4.3 340.1 %conditional.1 = ((bf16[448,1024]{1,0:T(8,128)(2,1)}, bf16[1,448,2048]{2,1,0:T(8,128)(2,1)}, bf16[1,448,2048]{2,1,0:T(8,128)(2,1)}, bf16[1,448,2048]{2,1,0:T(8,128)(2,1)})) conditional(s32[]{:T(128)} %clamp.3, (s32[8,1024]{1,0:T(8,128)}, f32[8,1024]{1,0:T(8,128)}, s32[16]{0:T(128)}, s32[16]{0:T(128)}, bf16[448,1024]{1,0:T(8,128)(2,1)}, ...), branch_computations={%region_4.5_spmd, %region_5.6_spmd} | conditional | bytes 8 | solution.py:632
  4.5 339.9 %moe_swap_any.1 = (bf16[448,1024]{1,0:T(8,128)(2,1)}, bf16[1,448,2048]{2,1,0:T(8,128)(2,1)}, bf16[1,448,2048]{2,1,0:T(8,128)(2,1)}, bf16[1,448,2048]{2,1,0:T(8,128)(2,1)}) custom-call(s32[8,1024]{1,0:T(8,128)} %get-tuple-element.40.refs_0_, f32[8,1024]{1,0:T(8,128)} %get-tuple-element.41.refs_1_, s32[16]{0:T(128)} %get-tuple-element.42.refs_2_, ...), custom_call_target="tpu_custom_call" | custom-call | tf_op jit(solution)/shard_map/cond/branch_1_fun/moe_swap_any/pallas_call | solution.py:588
  344.5 0.0 copy-start
  344.5 2.3 copy.24
  346.8 0.0 copy-done
  346.8 0.0 copy-start.1
  346.8 1.2 copy.25
  348.0 0.9 copy-done.1
  348.9 0.0 copy-start.2
  348.9 1.2 copy.26
  350.2 0.9 copy-done.2
  351.1 1.2 copy.27
  (1 shorter events, 0.0 us)
Async XLA Ops:
  344.5 2.3 copy-start
  346.8 2.2 copy-start.1
  348.9 2.2 copy-start.2

commit v4 on v3

--- a/solution.py
+++ b/solution.py
@@ -18,7 +18,7 @@
 ROWS = (((0,), (0,)), ((), ()))
 EARLY = 4
 SWAP_REFS = {True: 6, False: 13}
-PLANS = ((1, 1), None)
+PLANS = ((1, 1), (2, 0), None)
 
 
 def iota(shape, axis):
@@ -89,7 +89,7 @@
 
 
 def row_swap(
-    plan, me, partner, weights, placed, q0, q1, q2, e0, e1, e2, zsend, relay, xsend, xrelay, local_sem, ss, rs
+    plan, me, partner, weights, placed, q0, q1, q2, e0, e1, e2, sbuf, relay, x1relay, x2relay, local_sem, ss, rs
 ):
     near, far = plan
     row_box, far_box = (q0, q1, q2), (e0, e1, e2)
@@ -106,6 +106,10 @@
     def part(ref, j):
         return ref.at[0, :, pl.ds(pl.multiple_of(j * quarter, quarter), quarter)]
 
+    def cut(ref, j, w):
+        size = quarter // 2
+        return ref.at[0, :, pl.ds(pl.multiple_of(j * quarter + w * size, size), size)]
+
     def row_at(i):
         return lax.div(partner[i], 4)
 
@@ -128,10 +132,24 @@
         return d == 0, si, jnp.minimum(place, e0.shape[0] - 1)
 
     def x1(n, sender=False):
-        ways = ((xp, xm), (xm, xp), (xo, xo))
         return [
             rcopy(part(weights[n], to), row_box[n].at[x if sender else src], ss.at[n, d], rs.at[n, d], at(r, to))
-            for d, (to, src) in enumerate(ways)
+            for d, (to, src) in enumerate(((xp, xm), (xm, xp)))
+        ]
+
+    def x1_first(n):
+        return [
+            rcopy(cut(weights[n], xo, w), x1relay.at[n, w], ss.at[n, 2 + w], rs.at[n, 2 + w], at(r, to))
+            for w, to in enumerate((xp, xm))
+        ]
+
+    def x1_last(n, sender=False):
+        return [
+            rcopy(
+                x1relay.at[n, w], row_box[n].at[src if sender else xo, :, side],
+                ss.at[n, 4 + w], rs.at[n, 4 + w], at(r, to),
+            )
+            for w, (to, src, side) in enumerate(((xp, xm, left), (xm, xp, right)))
         ]
 
     def x1_local(n):
@@ -141,13 +159,13 @@
         out = []
         if group:
             for k in range(near):
-                out.append((zsend.at[n, k], far_box[n].at[k], rp))
-                out.append((zsend.at[n, near + k], far_box[n].at[near + k], rm))
+                out.append((sbuf.at[n, k], far_box[n].at[k], rp))
+                out.append((sbuf.at[n, near + k], far_box[n].at[near + k], rm))
         else:
             for k in range(far):
-                out.append((zsend.at[n, 2 * near + k, :, left], relay.at[n, 0, k], rp))
-                out.append((zsend.at[n, 2 * near + k, :, right], relay.at[n, 1, k], rm))
-        first = 3 + 2 * far * group
+                out.append((sbuf.at[n, 2 * near + k, :, left], relay.at[n, 0, k], rp))
+                out.append((sbuf.at[n, 2 * near + k, :, right], relay.at[n, 1, k], rm))
+        first = 6 + 2 * far * group
         return [
             rcopy(a, b, ss.at[n, first + i], rs.at[n, first + i], at(row, x)) for i, (a, b, row) in enumerate(out)
         ]
@@ -164,89 +182,114 @@
 
     def x2(n, sender=False):
         return [
-            rcopy(xsend.at[n, 1], part(placed[n], x if sender else xm), ss.at[n, 26], rs.at[n, 26], at(r, xp)),
-            rcopy(xsend.at[n, 2], part(placed[n], x if sender else xp), ss.at[n, 27], rs.at[n, 27], at(r, xm)),
+            rcopy(
+                sbuf.at[n, 1 + d], part(placed[n], x if sender else src),
+                ss.at[n, 22 + d], rs.at[n, 22 + d], at(r, to),
+            )
+            for d, (to, src) in enumerate(((xp, xm), (xm, xp)))
         ]
 
     def x2_first(n):
-        return rcopy(xsend.at[n, 3], xrelay.at[n], ss.at[n, 28], rs.at[n, 28], at(r, xm))
+        return [
+            rcopy(sbuf.at[n, 3, :, side], x2relay.at[n, w], ss.at[n, 24 + w], rs.at[n, 24 + w], at(r, to))
+            for w, (to, side) in enumerate(((xp, left), (xm, right)))
+        ]
 
     def x2_last(n, sender=False):
-        return rcopy(
-            xrelay.at[n], part(placed[n], xp if sender else xo), ss.at[n, 29], rs.at[n, 29], at(r, xm)
-        )
+        return [
+            rcopy(
+                x2relay.at[n, w], cut(placed[n], src if sender else xo, w),
+                ss.at[n, 26 + w], rs.at[n, 26 + w], at(r, to),
+            )
+            for w, (to, src) in enumerate(((xp, xm), (xm, xp)))
+        ]
 
     def x2_local(n):
-        return pltpu.make_async_copy(xsend.at[n, 0], part(placed[n], x), local_sem.at[3 + n])
+        return pltpu.make_async_copy(sbuf.at[n, 0], part(placed[n], x), local_sem.at[3 + n])
 
     def x1_send(n):
-        for c in x1(n, True):
+        for c in x1_first(n) + x1(n, True):
             c.start()
         x1_local(n).start()
 
+    def x1_relay(n):
+        for c, d in zip(x1_first(n), x1_last(n, True)):
+            c.wait_recv()
+            d.start()
+
     def z1_send(n):
-        for c in x1(n):
+        for c in x1(n) + x1_last(n):
             c.wait_recv()
         x1_local(n).wait()
         for k in range(far):
-            zsend[n, 2 * near + k] = row_box[n][find(lax.rem(r + 2, 4), k)]
+            sbuf[n, 2 * near + k] = row_box[n][find(lax.rem(r + 2, 4), k)]
         for k in range(near):
-            zsend[n, k] = row_box[n][find(rp, k)]
-            zsend[n, near + k] = row_box[n][find(rm, k)]
+            sbuf[n, k] = row_box[n][find(rp, k)]
+            sbuf[n, near + k] = row_box[n][find(rm, k)]
         for c in z1(n, 0) + z1(n, 1):
             c.start()
 
     def z2_send(n):
-        for c in z1(n, 0):
+        for c, d in zip(z1(n, 0), z2(n)):
             c.wait_recv()
-        for c in z2(n):
-            c.start()
+            d.start()
 
     def x2_send(n):
         for c in z1(n, 1) + z2(n):
             c.wait_recv()
+        for c in z1(n, 0) + z1(n, 1):
+            c.wait_send()
         for j, col in enumerate((x, xp, xm, xo)):
             stays, si, place = held(col)
-            xsend[n, j] = jnp.where(stays, row_box[n][si], far_box[n][place])
-        for c in [x2_first(n)] + x2(n, True):
+            sbuf[n, j] = jnp.where(stays, row_box[n][si], far_box[n][place])
+        for c in x2_first(n) + x2(n, True):
             c.start()
         x2_local(n).start()
 
     def x2_relay(n):
-        x2_first(n).wait_recv()
-        x2_last(n, True).start()
+        for c, d in zip(x2_first(n), x2_last(n, True)):
+            c.wait_recv()
+            d.start()
 
     def finish(n):
-        for c in x2(n):
+        for c in x2(n) + x2_last(n):
             c.wait_recv()
-        x2_last(n).wait_recv()
         x2_local(n).wait()
-        for c in x1(n, True) + z1(n, 0) + z1(n, 1) + z2(n) + x2(n, True) + [x2_first(n), x2_last(n, True)]:
+        for c in x1_first(n) + x1(n, True) + x1_last(n, True) + z2(n):
+            c.wait_send()
+        for c in x2_first(n) + x2(n, True) + x2_last(n, True):
             c.wait_send()
 
     def swap(point):
         if point == 0:
             x1_send(0)
+        if point == 10:
+            x1_relay(0)
         if point == 1:
             x1_send(1)
-            x1_send(2)
         if point == 2:
             z1_send(0)
+            x1_relay(1)
+            x1_send(2)
+            z1_send(1)
         if point == 3:
-            z1_send(1)
+            x1_relay(2)
+        if point == 4:
+            z2_send(0)
+        if point == 11:
+            z2_send(1)
         if point == 6:
-            z2_send(0)
             z1_send(2)
-            z2_send(1)
+            x2_send(0)
+        if point == 7:
+            x2_send(1)
+            z2_send(2)
         if point == 8:
-            x2_send(0)
-            z2_send(2)
-            x2_send(1)
             x2_relay(0)
+            x2_relay(1)
+            x2_send(2)
+            x2_relay(2)
         if point == 9:
-            x2_send(2)
-            for n in range(1, 3):
-                x2_relay(n)
             for n in range(3):
                 finish(n)
 
@@ -361,6 +404,7 @@
 
         return 0
 
+    swap(10)
     lax.fori_loop(0, N, dispatch, 0)
 
     swap(1)
@@ -448,7 +492,6 @@
         c = rcopy(y2s.at[w], y2r.at[w], dss.at[3 + w], drs.at[3 + w], dev)
         c.start()
         y2.append(c)
-    swap(5)
     for w in range(2):
         acc[w, :, cols(yy, 256)] = block(w, yy) + y1r[w, 0].astype(F32)
     for w in range(2):
@@ -461,6 +504,7 @@
         acc[w, :, here] = acc[w, :, here] + jnp.where(zl == 0, lo, hi)
     to_z = rcopy(zs, zr, dss.at[5], drs.at[5], dev_z)
     to_z.start()
+    swap(11)
     to_z.wait_recv()
     here = pl.ds(pl.multiple_of(yy * 256 + zl * 128, 128), 128)
     gsum = acc[0, :, here] + zr[0].astype(F32)
@@ -581,8 +625,8 @@
         half = max(far, 1)
         swap_scratch = [
             *[V((4, width, quarter), BF16)] * 3, *[V((2 * near + far, width, quarter), BF16)] * 3,
-            V((3, 2 * near + far, width, quarter), BF16),
-            V((3, 2, half, width, quarter // 2), BF16), V((3, 4, width, quarter), BF16), V((3, width, quarter), BF16),
+            V((3, max(2 * near + far, 4), width, quarter), BF16), V((3, 2, half, width, quarter // 2), BF16),
+            V((3, 2, width, quarter // 2), BF16), V((3, 2, width, quarter // 2), BF16),
             D((6,)), D((3, 32)), D((3, 32)),
         ]
     return pl.pallas_call(

time: 353 us -> 241 us (0.68)
  the two profiles are of different devices: /device:TPU:57 before, /device:TPU:17 now
where the time goes in v4:
time: 241 us; the launch traced here: 240 us
  Pallas kernels  227 us (94%)
  local copies, waits for them, and re-layouts  8.01 us (3%)
  between operations  3.27 us (1%)
    pallas_call x1, Pallas kernels, layer(): pl.pallas_call(functools.partial(kernel, plan), out_shape=(jax.ShapeDtype...  227 us
    unnamed x10, local copies, waits for them, and re-layouts  7.85 us

profile of v4, /device:TPU:17, one launch (start us, length us, event | category | flops | bytes accessed | tf_op | source)
XLA Modules:
  0.0 240.5 jit_solution(2941421838436221758)
XLA Ops:
  0.6 0.7 compare_convert_fusion
  1.3 0.1 reshape.17
  1.4 0.1 reduce_sum.18
  1.5 0.6 reduce_max.18
  3.5 0.1 reshape.18
  3.5 0.1 reduce_sum.19
  3.7 0.6 reduce_max.19
  5.6 227.0 %conditional.1 = ((bf16[448,1024]{1,0:T(8,128)(2,1)}, bf16[1,448,2048]{2,1,0:T(8,128)(2,1)}, bf16[1,448,2048]{2,1,0:T(8,128)(2,1)}, bf16[1,448,2048]{2,1,0:T(8,128)(2,1)})) conditional(s32[]{:T(128)} %clamp.3, (s32[8,1024]{1,0:T(8,128)}, f32[8,1024]{1,0:T(8,128)}, s32[16]{0:T(128)}, s32[16]{0:T(128)}, bf16[448,1024]{1,0:T(8,128)(2,1)}, ...), branch_computations={%region_4.5_spmd, %region_5.6_spmd, %region_6.7_spmd} | conditional | bytes 8 | solution.py:676
  5.6 226.7 %moe_swap_11.1 = (bf16[448,1024]{1,0:T(8,128)(2,1)}, bf16[1,448,2048]{2,1,0:T(8,128)(2,1)}, bf16[1,448,2048]{2,1,0:T(8,128)(2,1)}, bf16[1,448,2048]{2,1,0:T(8,128)(2,1)}) custom-call(s32[8,1024]{1,0:T(8,128)} %get-tuple-element.48.refs_0_, f32[8,1024]{1,0:T(8,128)} %get-tuple-element.49.refs_1_, s32[16]{0:T(128)} %get-tuple-element.50.refs_2_, ...), custom_call_target="tpu_custom_call" | custom-call | tf_op jit(solution)/shard_map/cond/branch_0_fun/moe_swap_11/pallas_call | solution.py:632
  232.6 0.0 copy-start
  232.6 2.3 copy.28
  234.9 0.0 copy-done
  234.9 0.0 copy-start.1
  234.9 1.2 copy.29
  236.2 0.9 copy-done.1
  237.1 0.0 copy-start.2
  237.1 1.2 copy.30
  238.3 0.9 copy-done.2
  239.3 1.2 copy.31
  (1 shorter events, 0.0 us)
Async XLA Ops:
  232.6 2.3 copy-start
  234.9 2.2 copy-start.1
  237.1 2.2 copy-start.2
